TPU v7x, 256 devices: a whole 4x4x8 slice. The times are simulated.
256 devices in a mesh: grp: 16 (over z, core), pts: 16 (over y, x).
Axes of the slice: x: 4, y: 4, z: 8, core: 2. Of those that a mesh axis runs over, the one named last changes fastest.
Arguments:
- patches: bfloat16 [16, 16, 16384, 128], P('grp', 'pts'), may hold values from -6 to 6
- counts: int32 [16, 16], replicated, may hold values from 1 to 16384, as said below
- pick_slot: int32 [3, 128], replicated, may hold values from 0 to 16383, as said below
- block_owner: int32 [3], replicated, may hold values from 0 to 255, as said below
Outputs:
- factor_rows: bfloat16 [16, 16, 8192, 384], P('grp', 'pts')
- residual_gain: float32 [16, 16, 8192], P('grp', 'pts')
Inputs may be any that keep to these rules, and one draw needn't show every extreme that they name: `counts`: each row sums to 131072, and in every row one device holds exactly 16384; in the last row it is the last column. `pick_slot`: the 128 slots of round r are distinct and below the count of block_owner[r]; the round owned by the last device includes slot 16383. `block_owner`: the owners of the rounds are distinct devices, and one of them is the last device.
All inputs are finite; a program needn't handle non-finite values.
Results may differ from a plain program's by a relative error of at most 0.0075.
Values may be sent and summed in bfloat16 or wider, within the bound.
A program may use at most 192 MiB of HBM per device.

v0:
```python
import jax
import jax.numpy as jnp
from jax import lax
from jax.sharding import PartitionSpec as P

PTS_DEV = 8192


JITTER = 0.1
HIGHEST = lax.Precision.HIGHEST


def from_root(block, axis, holder):
    block = jnp.where(lax.axis_index(axis) == holder, block, jnp.zeros_like(block))
    return lax.psum(block, axis)


def squares(matrix):
    return jnp.sum(jnp.square(matrix.astype(jnp.float32)), axis=1)


def affinity(row_data, rows_sq, row_ids, block_rows, block_sq, block_ids):
    cross_dot = lax.dot_general(
        row_data, block_rows, (((1,), (1,)), ((), ())), preferred_element_type=jnp.float32
    )
    inverse_scale = 1.0 / row_data.shape[1]
    distance = rows_sq[:, None] + block_sq[None, :] - 2.0 * cross_dot
    same_point = (row_ids[:, None] == block_ids[None, :]).astype(jnp.float32)
    return jnp.exp(-inverse_scale * distance) + JITTER * same_point


def extend(factors, kernel_part, cross_rows, inverse):
    if factors.shape[1] > 0:
        kernel_part = kernel_part - lax.dot_general(
            factors,
            cross_rows,
            (((1,), (1,)), ((), ())),
            precision=HIGHEST,
            preferred_element_type=jnp.float32,
        )
    fresh_rows = lax.dot_general(
        kernel_part,
        inverse,
        (((1,), (1,)), ((), ())),
        precision=HIGHEST,
        preferred_element_type=jnp.float32,
    )
    return jnp.concatenate([factors, fresh_rows], axis=1)


def prepare(blocks, block_ids):
    round_count, block_size = block_ids.shape
    stacked = blocks.reshape(round_count * block_size, blocks.shape[2])
    stacked_ids = block_ids.reshape(-1)
    stacked_sq = squares(stacked)
    factors = jnp.zeros((round_count * block_size, 0), jnp.float32)
    identity = jnp.eye(block_size, dtype=jnp.float32)
    inverses = []
    crosses = []
    for step_index in range(round_count):
        lower_edge = step_index * block_size
        cross_rows = factors[lower_edge : lower_edge + block_size]
        block_sq = stacked_sq[lower_edge : lower_edge + block_size]
        schur_block = affinity(
            blocks[step_index],
            block_sq,
            block_ids[step_index],
            blocks[step_index],
            block_sq,
            block_ids[step_index],
        )
        if step_index > 0:
            schur_block = schur_block - lax.dot_general(
                cross_rows,
                cross_rows,
                (((1,), (1,)), ((), ())),
                precision=HIGHEST,
                preferred_element_type=jnp.float32,
            )
        factor_low = jnp.linalg.cholesky(schur_block)
        inverse = lax.linalg.triangular_solve(factor_low, identity, left_side=True, lower=True)
        kernel_part = affinity(
            stacked, stacked_sq, stacked_ids, blocks[step_index], block_sq, block_ids[step_index]
        )
        factors = extend(factors, kernel_part, cross_rows, inverse)
        inverses.append(inverse)
        crosses.append(cross_rows)
    return (inverses, crosses)


def factorize(row_data, row_ids, blocks, block_ids, inverses, crosses):
    rows_sq = squares(row_data)
    blocks_sq = squares(blocks.reshape(-1, blocks.shape[2])).reshape(block_ids.shape)
    factors = jnp.zeros((row_data.shape[0], 0), jnp.float32)
    for step_index in range(len(inverses)):
        kernel_part = affinity(
            row_data,
            rows_sq,
            row_ids,
            blocks[step_index],
            blocks_sq[step_index],
            block_ids[step_index],
        )
        factors = extend(factors, kernel_part, crosses[step_index], inverses[step_index])
    point_gains = 1.0 + JITTER - jnp.sum(factors * factors, axis=1)
    return (factors, point_gains)


def per_device(patches, counts, pick_slot, block_owner):
    groups = lax.axis_size("grp")
    columns = lax.axis_size("pts")
    my_group = lax.axis_index("grp")
    my_column = lax.axis_index("pts")
    local_rows = patches[0, 0]
    slot_count = local_rows.shape[0]
    embed_width = local_rows.shape[1]
    per_peer = slot_count // groups
    round_count, block_size = pick_slot.shape
    ends_table = jnp.cumsum(counts, axis=1)
    starts_table = ends_table - counts
    col_ends = lax.dynamic_index_in_dim(ends_table, my_column, 0, keepdims=False)
    col_starts = lax.dynamic_index_in_dim(starts_table, my_column, 0, keepdims=False)
    my_start = lax.dynamic_index_in_dim(col_starts, my_group, 0, keepdims=False)
    my_count = lax.dynamic_index_in_dim(col_ends, my_group, 0, keepdims=False) - my_start
    target = jnp.arange(groups, dtype=jnp.int32)[:, None]
    offsets = (target - my_start) % groups + jnp.arange(per_peer, dtype=jnp.int32)[None, :] * groups
    in_range = offsets < my_count
    take_rows = jnp.minimum(offsets, slot_count - 1).reshape(-1)
    slot_rank = jnp.arange(PTS_DEV, dtype=jnp.int32) * groups + my_group
    sources = jnp.sum((col_ends[None, :] <= slot_rank[:, None]).astype(jnp.int32), axis=1)
    begin_slot = (col_starts + (my_group - col_starts) % groups) // groups
    source_hit = jnp.arange(groups, dtype=jnp.int32)[None, :] == sources[:, None]
    source_begin = jnp.sum(jnp.where(source_hit, begin_slot[None, :], 0), axis=1)
    take_index = sources * per_peer + jnp.arange(PTS_DEV, dtype=jnp.int32) - source_begin
    owner_group = block_owner // columns
    owner_column = block_owner % columns
    pick_rank = starts_table[owner_column, owner_group][:, None] + pick_slot
    block_ids = (
        pick_rank % groups * columns + owner_column[:, None]
    ) * PTS_DEV + pick_rank // groups
    chosen = jnp.take(local_rows, pick_slot.reshape(-1), axis=0).reshape(
        round_count, block_size, embed_width
    )
    fetched = []
    for step_index in range(round_count):
        fetched.append(from_root(chosen[step_index], ("grp", "pts"), block_owner[step_index]))
    blocks = jnp.stack(fetched)
    inverses, crosses = prepare(blocks, block_ids)
    shaped = jnp.take(local_rows, take_rows, axis=0).reshape(
        (groups, per_peer) + local_rows.shape[1:]
    )
    keep_mask = in_range.reshape((groups, per_peer) + (1,) * (local_rows.ndim - 1))
    received = lax.all_to_all(
        jnp.where(keep_mask, shaped, jnp.zeros((), local_rows.dtype)),
        "grp",
        split_axis=0,
        concat_axis=0,
        tiled=True,
    )
    flat_rows = received.reshape((groups * per_peer,) + received.shape[2:])
    points = jnp.take(flat_rows, take_index, axis=0)
    point_ids = (my_group * columns + my_column) * PTS_DEV + jnp.arange(PTS_DEV, dtype=jnp.int32)
    factors, point_gains = factorize(points, point_ids, blocks, block_ids, inverses, crosses)
    factor_rows = factors.astype(jnp.bfloat16)
    return (factor_rows[None, None], point_gains[None, None])


def solution(mesh):
    in_specs = (P("grp", "pts", None, None), P(), P(), P())
    out_specs = (P("grp", "pts", None, None), P("grp", "pts", None))
    return jax.shard_map(
        per_device, mesh=mesh, in_specs=in_specs, out_specs=out_specs, check_vma=False
    )
```

profile of v0, /device:TPU:1, one launch (start us, length us, event | category | flops | bytes accessed | tf_op | source)
XLA Modules:
  0.0 556.6 jit_solution(17895677158123767266)
XLA Ops:
  7.2 0.9 reduce_window_sum.11
  8.0 0.7 sub.107
  12.2 58.2 %gather_fusion = bf16[16384,128]{1,0:T(8,128)(2,1)} fusion(bf16[16384,128]{1,0:T(8,128)(2,1)} %bitcast.108, s32[16384]{0:T(1024)S(1)} %broadcast_clamp_fusion), kind=kCustom, calls=%fused_computation | custom fusion | bytes 8454144 | tf_op jit(solution)/shard_map/jit(_take)/gather | solution.py:149
  70.4 7.6 %select_select_fusion = bf16[16,1024,128]{2,1,0:T(8,128)(2,1)} fusion(bf16[16,1024,128]{2,1,0:T(8,128)(2,1)} %bitcast.110, pred[16,1024]{1,0:T(8,128)(4,1)S(1)} %get-tuple-element.21, pred[16,1024]{1,0:T(8,128)(4,1)S(1)} %get-tuple-element.20), kind=kLoop, calls=%fused_computation.28 | loop fusion | flops 4194304 | bytes 8421376 | tf_op jit(solution)/shard_map/jit(_where)/select_n | solution.py:154
  78.0 10.1 %all-to-all-start = ((bf16[16,1024,128]{2,1,0:T(8,128)(2,1)}), bf16[16,1024,128]{2,1,0:T(8,128)(2,1)}, u32[]{:S(2)}, u32[]{:S(2)}) async-start(bf16[16,1024,128]{2,1,0:T(8,128)(2,1)} %select_select_fusion), calls=%async_computation | async-start | bytes 8388608 | tf_op jit(solution)/shard_map/all_to_all | solution.py:153
  90.8 4.2 gather_fusion.2
  97.2 284.3 %all-reduce.3.cloned.1.call-done = (bf16[128,128]{1,0:T(8,128)(2,1)}, bf16[128,128]{1,0:T(8,128)(2,1)}, bf16[128,128]{1,0:T(8,128)(2,1)}) async-done(((bf16[128,128]{1,0:T(8,128)(2,1)}, bf16[128,128]{1,0:T(8,128)(2,1)}, bf16[128,128]{1,0:T(8,128)(2,1)}), (bf16[128,128]{1,0:T(8,128)(2,1)}, bf16[128,128]{1,0:T(8,128)(2,1)}, bf16[128,128]{1,0:T(8,128)(2,1)})) %all-reduce.3.cloned.1.call-update) | async-done | bytes 98320 | tf_op jit(solution)/shard_map/psum | solution.py:15
  381.5 0.9 multiply_reduce_fusion.1
  382.4 1.0 fusion.36
  383.5 11.7 %cholesky.59 = f32[128,128]{1,0:T(8,128)S(1)} custom-call(f32[128,128]{1,0:T(8,128)S(1)} %fusion.54), custom_call_target="Cholesky" | custom-call | tf_op jit(solution)/shard_map/jit(cholesky)/cholesky | solution.py:80
  396.6 9.8 %custom-call.9 = f32[1,128,128]{1,2,0:T(8,128)S(1)} custom-call(f32[1,128,128]{2,1,0:T(8,128)S(1)} %fusion.46), custom_call_target="InvertDiagBlocksLowerTriangular" | custom-call | tf_op jit(solution)/shard_map/triangular_solve/custom-call.0 | solution.py:81
  406.7 1.0 fusion.32
  407.7 1.0 fusion.19
  409.5 11.7 %cholesky.70 = f32[128,128]{1,0:T(8,128)S(1)} custom-call(f32[128,128]{1,0:T(8,128)S(1)} %fusion.52), custom_call_target="Cholesky" | custom-call | tf_op jit(solution)/shard_map/jit(cholesky)/cholesky | solution.py:80
  422.5 10.3 %custom-call.10 = f32[1,128,128]{1,2,0:T(8,128)S(1)} custom-call(f32[1,128,128]{2,1,0:T(8,128)S(1)} %fusion.47), custom_call_target="InvertDiagBlocksLowerTriangular" | custom-call | tf_op jit(solution)/shard_map/triangular_solve/custom-call.0 | solution.py:81
  433.1 1.0 fusion.28
  434.6 1.0 fusion.24
  436.5 11.7 %cholesky.81 = f32[128,128]{1,0:T(8,128)S(1)} custom-call(f32[128,128]{1,0:T(8,128)S(1)} %fusion.50), custom_call_target="Cholesky" | custom-call | tf_op jit(solution)/shard_map/jit(cholesky)/cholesky | solution.py:80
  449.6 9.8 %custom-call.11 = f32[1,128,128]{1,2,0:T(8,128)S(1)} custom-call(f32[1,128,128]{2,1,0:T(8,128)S(1)} %fusion.48), custom_call_target="InvertDiagBlocksLowerTriangular" | custom-call | tf_op jit(solution)/shard_map/triangular_solve/custom-call.0 | solution.py:81
  459.7 24.6 %gather_fusion.1 = bf16[8192,128]{1,0:T(8,128)(2,1)S(1)} fusion(bf16[16384,128]{1,0:T(8,128)(2,1)} %bitcast.7, s32[8192]{0:T(1024)S(1)} %broadcast_clamp_fusion.1), kind=kCustom, calls=%fused_computation.1 | custom fusion | bytes 4227072 | tf_op jit(solution)/shard_map/jit(_take)/gather | solution.py:161
  484.3 2.7 multiply_reduce_fusion
  487.1 3.3 fusion.6
  490.4 3.3 fusion.9
  493.8 3.3 fusion.12
  497.1 4.4 fusion.78
  501.6 6.7 %convolution_subtract_fusion.1 = f32[8192,128]{1,0:T(8,128)S(1)} fusion(f32[8192,128]{1,0:T(8,128)S(1)} %fusion.9, f32[8192,128]{0,1:T(8,128)S(1)} %fusion.78, f32[384,128]{0,1:T(8,128)S(1)} %fusion.79), kind=kOutput, calls=%fused_computation.9 | convolution fusion | flops 1611661312 | bytes 12648448 | tf_op jit(solution)/shard_map/dot_general | solution.py:34
  508.2 4.6 fusion.80
  512.9 14.2 %convolution_subtract_fusion = f32[8192,128]{1,0:T(8,128)S(1)} fusion(f32[8192,128]{1,0:T(8,128)S(1)} %fusion.12, f32[8192,128]{0,1:T(8,128)S(1)} %fusion.80, f32[8192,128]{0,1:T(8,128)S(1)} %fusion.78, f32[384,128]{0,1:T(8,128)S(1)} %fusion.81, f32[384,128]{0,1:T(8,128)S(1)} %fusion.79), kind=kOutput, calls=%fused_computation.6 | convolution fusion | flops 3224403968 | bytes 17170432 | tf_op jit(solution)/shard_map/dot_general | solution.py:34
  527.1 4.1 fusion.82
  531.2 1.4 fusion
  534.0 7.0 %pad_maximum_fusion = bf16[1,1,8192,384]{2,3,1,0:T(8,128)(2,1)} fusion(bf16[1,1,8192,128]{2,3,1,0:T(8,128)(2,1)S(1)} %convert_bitcast_fusion, bf16[1,1,8192,128]{2,3,1,0:T(8,128)(2,1)S(1)} %convert_bitcast_fusion.1, bf16[1,1,8192,128]{2,3,1,0:T(8,128)(2,1)S(1)} %convert_bitcast_fusion.2), kind=kLoop, calls=%fused_computation.26 | loop fusion | flops 18874368 | bytes 12582912 | tf_op jit(solution)/shard_map/concatenate | solution.py:48
  541.0 8.6 %copy.32 = bf16[1,1,8192,384]{3,2,1,0:T(8,128)(2,1)} copy(bf16[1,1,8192,384]{2,3,1,0:T(8,128)(2,1)} %pad_maximum_fusion) | data formatting | bytes 12582912
  (70 shorter events, 13.4 us)
Async XLA Ops:
  78.0 10.2 %copy-start.4 = (s32[3]{0:T(128)S(1)}, s32[3]{0:T(128)}, u32[]{:S(2)}) copy-start(s32[3]{0:T(128)} %param.10) | copy-start | bytes 40
  78.0 12.7 %copy-start.3 = (s32[3,128]{1,0:T(4,128)S(1)}, s32[3,128]{1,0:T(4,128)}, u32[]{:S(2)}) copy-start(s32[3,128]{1,0:T(4,128)} %param.9) | copy-start | bytes 4612
  78.0 381.7 %all-to-all-start = ((bf16[16,1024,128]{2,1,0:T(8,128)(2,1)}), bf16[16,1024,128]{2,1,0:T(8,128)(2,1)}, u32[]{:S(2)}, u32[]{:S(2)}) async-start(bf16[16,1024,128]{2,1,0:T(8,128)(2,1)} %select_select_fusion), calls=%async_computation | async-start | bytes 8388608 | tf_op jit(solution)/shard_map/all_to_all | solution.py:153
  88.2 293.3 %all-reduce.3.cloned.1.call-start = ((), (), s32[]{:S(2)}) async-start(), calls=%async_computation.1 | async-start | bytes 196608 | tf_op jit(solution)/shard_map/psum | solution.py:15
  459.7 27.4 %copy-start.2 = (bf16[128,128]{1,0:T(8,128)(2,1)S(1)}, bf16[128,128]{1,0:T(8,128)(2,1)}, u32[]{:S(2)}) copy-start(bf16[128,128]{1,0:T(8,128)(2,1)} %get-tuple-element.12) | copy-start | bytes 98308
  487.1 3.3 copy-start.1
  490.4 3.3 copy-start
Sparse Core Ops, SparseCore 0:
  95.9 285.5 all-reduce.2
where the time goes:
time: 560 us; the launch traced here: 557 us
  waiting for transfers between devices  284 us (51%)
  local copies, waits for them, and re-layouts  98.4 us (18%)
  other arithmetic  94 us (17%)
  matrix products  51.8 us (9%)
  between operations  17.9 us (3%)
  starting transfers between devices  10.2 us (2%)
    psum x1, waiting for transfers between devices, from_root(): return lax.psum(block, axis)  284 us
    gather x1, local copies, waits for them, and re-layouts, per_device(): jnp.take(local_rows, take_rows, axis=0)  58.2 us
    another operation x9, other arithmetic, prepare(): factor_low = jnp.linalg.cholesky(schur_block)  37.2 us
    another operation x6, other arithmetic, prepare(): lax.linalg.triangular_solve(factor_low, identity, left_side=True, lower=T...  31.9 us
    gather x1, local copies, waits for them, and re-layouts, per_device(): points = jnp.take(flat_rows, take_index, axis=0)  24.6 us
    dot_general x3, matrix products, extend(): lax.dot_general(factors, cross_rows, (((1,), (1,)), ((), ())), precision=...  21.4 us
    dot_general x8, matrix products, affinity(): lax.dot_general(row_data, block_rows, (((1,), (1,)), ((), ())), preferred...  14.9 us
    dot_general x5, matrix products, extend(): lax.dot_general(kernel_part, inverse, (((1,), (1,)), ((), ())), precision...  14 us
  transfers between devices with their start and end apart: 2, of which 1 were waited for; matrix products, arithmetic and copies ran while one was open for 15% of the time, Pallas kernels for 0%

commit v1 on v0

v1 whole, which is shorter than its diff:
```python
import functools
import math

import jax
import jax.numpy as jnp
from jax import lax
from jax.experimental import pallas as pl
from jax.experimental.pallas import tpu as pltpu
from jax.sharding import PartitionSpec as P

MESH = pl.DeviceIdType.MESH
HIGHEST = lax.Precision.HIGHEST
JITTER = 0.1
EMBED = 128
BLOCK = 128
ROUNDS = 3
FACTOR = ROUNDS * BLOCK
PARTS = 12
PART_ROWS = FACTOR // PARTS
EXP_SCALE = math.log2(math.e) / EMBED
F32 = jnp.float32
BF16 = jnp.bfloat16


def dot(a, b, precision=None):
    return jnp.dot(a, b, precision=precision, preferred_element_type=F32)


def dot_nt(a, b, precision=None):
    return lax.dot_general(
        a, b, (((1,), (1,)), ((), ())), precision=precision, preferred_element_type=F32
    )


def halves(x):
    high = x.astype(BF16)
    return high, (x - high.astype(F32)).astype(BF16)


def pack_kernel(n_grp, n_pts, counts, owner, slot_ref, x_ref, out_ref, picks_ref, wide, column, total):
    step = pl.program_id(0)
    group, col = lax.axis_index("grp"), lax.axis_index("pts")
    me = group * n_pts + col
    rows = wide.shape[0]
    start = jnp.int32(0)
    for h in range(n_grp):
        start += jnp.where(h < group, counts[col, h], 0)
    wide[...] = x_ref[0, 0].astype(F32)
    for t in range(n_grp):
        first = (t - start) & (n_grp - 1)
        out_ref[t] = wide[pl.ds(first, rows // n_grp, stride=n_grp), :].astype(BF16)

    mine = (owner[0] == me) | (owner[1] == me) | (owner[2] == me)

    @pl.when(step == 0)
    def _():
        total[...] = jnp.zeros_like(total)
        for r in range(ROUNDS):

            @pl.when(owner[r] == me)
            def _():
                column[...] = jnp.broadcast_to(slot_ref[r : r + 1, :], (BLOCK, BLOCK)).T

    @pl.when(mine)
    def _():
        lane = lax.broadcasted_iota(jnp.int32, (BLOCK, BLOCK), 1)
        wanted = column[...] - step * rows
        acc = total[...]
        for c in range(rows // BLOCK):
            hit = (wanted == lane + c * BLOCK).astype(F32).astype(BF16)
            acc += dot(hit, x_ref[0, 0, c * BLOCK : (c + 1) * BLOCK, :])
        total[...] = acc

    @pl.when(step == pl.num_programs(0) - 1)
    def _():
        for r in range(ROUNDS):
            picks_ref[r] = jnp.where(owner[r] == me, total[...], 0.0).astype(BF16)


def pack(patches, counts, pick_slot, block_owner, n_grp, n_pts):
    slots = patches.shape[2]
    steps = 8
    rows = slots // steps
    return pl.pallas_call(
        functools.partial(pack_kernel, n_grp, n_pts),
        grid=(steps,),
        out_shape=(
            jax.ShapeDtypeStruct((n_grp, slots // n_grp, EMBED), BF16),
            jax.ShapeDtypeStruct((ROUNDS, BLOCK, EMBED), BF16),
        ),
        in_specs=[
            pl.BlockSpec(memory_space=pltpu.SMEM),
            pl.BlockSpec(memory_space=pltpu.SMEM),
            pl.BlockSpec((ROUNDS, BLOCK), lambda i: (0, 0)),
            pl.BlockSpec((1, 1, rows, EMBED), lambda i: (0, 0, i, 0)),
        ],
        out_specs=(
            pl.BlockSpec((n_grp, rows // n_grp, EMBED), lambda i: (0, i, 0)),
            pl.BlockSpec((ROUNDS, BLOCK, EMBED), lambda i: (0, 0, 0)),
        ),
        scratch_shapes=[
            pltpu.VMEM((rows, EMBED), F32),
            pltpu.VMEM((BLOCK, BLOCK), jnp.int32),
            pltpu.VMEM((BLOCK, EMBED), F32),
        ],
        name="pack",
    )(counts, block_owner, pick_slot, patches)


def spread_kernel(n_grp, n_pts, in_ref, out_ref, got1, got2, part, gathered, s1, r1, s2, r2, s3, r3):
    group, col = lax.axis_index("grp"), lax.axis_index("pts")
    barrier = pltpu.get_barrier_semaphore()
    for d in range(1, n_grp):
        pl.semaphore_signal(
            barrier, inc=1, device_id=(lax.rem(group + d, n_grp), col), device_id_type=MESH
        )
    for d in range(1, n_pts):
        pl.semaphore_signal(
            barrier, inc=1, device_id=(group, lax.rem(col + d, n_pts)), device_id_type=MESH
        )
    pl.semaphore_wait(barrier, n_grp + n_pts - 2)

    def scatter(d):
        target = lax.rem(group + d, n_grp)
        source = jnp.minimum(target, PARTS - 1)
        return target, pltpu.make_async_remote_copy(
            src_ref=in_ref.at[source],
            dst_ref=got1.at[d - 1],
            send_sem=s1.at[d],
            recv_sem=r1.at[d],
            device_id=(target, col),
            device_id_type=MESH,
        )

    def across(d):
        return pltpu.make_async_remote_copy(
            src_ref=part.at[0],
            dst_ref=got2.at[d - 1],
            send_sem=s2.at[d],
            recv_sem=r2.at[d],
            device_id=(group, lax.rem(col + d, n_pts)),
            device_id_type=MESH,
        )

    def gather(d, owner):
        return pltpu.make_async_remote_copy(
            src_ref=part.at[1],
            dst_ref=gathered.at[owner],
            send_sem=s3.at[d],
            recv_sem=r3.at[d],
            device_id=(lax.rem(group + d, n_grp), col),
            device_id_type=MESH,
        )

    for d in range(1, n_grp):
        target, copy = scatter(d)

        @pl.when(target < PARTS)
        def _():
            copy.start()

    @pl.when(group < PARTS)
    def _():
        for d in range(1, n_grp):
            scatter(d)[1].wait_recv()
        acc = in_ref[jnp.minimum(group, PARTS - 1)].astype(F32)
        for d in range(1, n_grp):
            acc += got1[d - 1].astype(F32)
        part[0] = acc.astype(BF16)
        for d in range(1, n_pts):
            across(d).start()
        for d in range(1, n_pts):
            across(d).wait_recv()
        acc = part[0].astype(F32)
        for d in range(1, n_pts):
            acc += got2[d - 1].astype(F32)
        part[1] = acc.astype(BF16)
        for d in range(1, n_grp):
            gather(d, group).start()
        gathered[group] = part[1]

    for d in range(1, n_grp):
        source = lax.rem(group + n_grp - d, n_grp)

        @pl.when(source < PARTS)
        def _():
            gather(d, source).wait_recv()

    out_ref[...] = gathered[...]

    for d in range(1, n_grp):
        target, copy = scatter(d)

        @pl.when(target < PARTS)
        def _():
            copy.wait_send()

    @pl.when(group < PARTS)
    def _():
        for d in range(1, n_pts):
            across(d).wait_send()
        for d in range(1, n_grp):
            gather(d, group).wait_send()


def spread(picks, n_grp, n_pts):
    shape = (PARTS, PART_ROWS, EMBED)
    return pl.pallas_call(
        functools.partial(spread_kernel, n_grp, n_pts),
        out_shape=jax.ShapeDtypeStruct(shape, BF16),
        in_specs=[pl.BlockSpec(memory_space=pltpu.VMEM)],
        out_specs=pl.BlockSpec(memory_space=pltpu.VMEM),
        scratch_shapes=[
            pltpu.VMEM((n_grp - 1,) + shape[1:], BF16),
            pltpu.VMEM((n_pts - 1,) + shape[1:], BF16),
            pltpu.VMEM((2,) + shape[1:], BF16),
            pltpu.VMEM(shape, BF16),
        ]
        + [pltpu.SemaphoreType.DMA((max(n_grp, n_pts),))] * 6,
        compiler_params=pltpu.CompilerParams(collective_id=0, has_side_effects=True),
        cost_estimate=pl.CostEstimate(flops=20_000_000_000, bytes_accessed=200_000, transcendentals=0),
        name="spread",
    )(picks.reshape(shape))


def unit_inverse(a_ref, m_ref):
    sub = lax.broadcasted_iota(jnp.int32, (8, BLOCK), 0)
    m_ref[...] = (
        lax.broadcasted_iota(jnp.int32, (BLOCK, BLOCK), 0)
        == lax.broadcasted_iota(jnp.int32, (BLOCK, BLOCK), 1)
    ).astype(F32)

    def row(x, k):
        return jnp.broadcast_to(x[k : k + 1, :], (8, BLOCK))

    for b in range(BLOCK // 8):
        low = 8 * b
        pa = a_ref[low : low + 8, :]
        pm = m_ref[low : low + 8, :]
        cols = [jnp.broadcast_to(pa[:, low + j : low + j + 1], (8, BLOCK)) for j in range(8)]
        pivots = jnp.ones((8, BLOCK), F32)
        inverses = pivots
        for k in range(8):
            pivot = row(cols[k], k)
            inverse = 1.0 / pivot
            pivots = jnp.where(sub == k, pivot, pivots)
            inverses = jnp.where(sub == k, inverse, inverses)
            if k < 7:
                f = jnp.where(sub > k, cols[k] * inverse, 0.0)
                for j in range(k + 1, 8):
                    cols[j] = cols[j] - f * row(cols[j], k)
                pa = pa - f * row(pa, k)
                pm = pm - f * row(pm, k)
        if b < BLOCK // 8 - 1:
            below = pa.T[low + 8 :, :]
            a_ref[low + 8 :, :] -= dot(below, pa * inverses, HIGHEST)
            m_ref[low + 8 :, :] -= dot(below, pm * inverses, HIGHEST)
        scale = lax.rsqrt(pivots)
        scale = scale * (1.5 - 0.5 * pivots * scale * scale)
        m_ref[low : low + 8, :] = pm * scale


def prepare_kernel(b_ref, high_ref, low_ref, twice_ref, shift_ref, schur, work, inv):
    blocks = b_ref[...]
    wide = blocks.astype(F32)
    sq_high, sq_low = halves(wide * wide)
    ones = jnp.ones((EMBED, BLOCK), BF16)
    sq_col = dot(sq_high, ones) + dot(sq_low, ones)
    row_ones = jnp.ones((8, EMBED), BF16)
    sq_row = (dot_nt(row_ones, sq_high) + dot_nt(row_ones, sq_low))[0:1, :]
    shift_ref[...] = -EXP_SCALE * sq_row
    twice_ref[...] = (2.0 * wide).T.astype(BF16)
    eye = (
        lax.broadcasted_iota(jnp.int32, (BLOCK, BLOCK), 0)
        == lax.broadcasted_iota(jnp.int32, (BLOCK, BLOCK), 1)
    )
    def span(i):
        return slice(i * BLOCK, (i + 1) * BLOCK)

    for i in range(ROUNDS):
        for j in range(i + 1):
            inner = dot_nt(blocks[span(i)], blocks[span(j)])
            dist = 2.0 * inner - sq_col[span(i)] - sq_row[:, span(j)]
            part = jnp.exp2(EXP_SCALE * dist)
            if i == j:
                part = part + jnp.where(eye, JITTER, 0.0)
            schur[i, j] = part

    for r in range(ROUNDS):
        work[...] = schur[r, r]
        unit_inverse(work, inv.at[r, r])
        for i in range(r + 1, ROUNDS):
            schur[i, r] = dot_nt(schur[i, r], inv[r, r], HIGHEST)
        for i in range(r + 1, ROUNDS):
            for j in range(r + 1, i + 1):
                schur[i, j] -= dot_nt(schur[i, r], schur[j, r], HIGHEST)

    inv[1, 0] = -dot(inv[1, 1], dot(schur[1, 0], inv[0, 0], HIGHEST), HIGHEST)
    inv[2, 1] = -dot(inv[2, 2], dot(schur[2, 1], inv[1, 1], HIGHEST), HIGHEST)
    inv[2, 0] = -dot(
        inv[2, 2],
        dot(schur[2, 0], inv[0, 0], HIGHEST) + dot(schur[2, 1], inv[1, 0], HIGHEST),
        HIGHEST,
    )
    for i in range(ROUNDS):
        for j in range(ROUNDS):
            if j <= i:
                high, low = halves(inv[i, j].T)
            else:
                high = low = jnp.zeros((BLOCK, BLOCK), BF16)
            high_ref[span(j), span(i)] = high
            low_ref[span(j), span(i)] = low


def prepare(blocks):
    square = (ROUNDS, ROUNDS, BLOCK, BLOCK)
    return pl.pallas_call(
        prepare_kernel,
        out_shape=(
            jax.ShapeDtypeStruct((FACTOR, FACTOR), BF16),
            jax.ShapeDtypeStruct((FACTOR, FACTOR), BF16),
            jax.ShapeDtypeStruct((EMBED, FACTOR), BF16),
            jax.ShapeDtypeStruct((1, FACTOR), F32),
        ),
        in_specs=[pl.BlockSpec(memory_space=pltpu.VMEM)],
        out_specs=(pl.BlockSpec(memory_space=pltpu.VMEM),) * 4,
        scratch_shapes=[
            pltpu.VMEM(square, F32),
            pltpu.VMEM((BLOCK, BLOCK), F32),
            pltpu.VMEM(square, F32),
        ],
        cost_estimate=pl.CostEstimate(flops=40_000_000_000, bytes_accessed=900_000, transcendentals=0),
        name="prepare",
    )(blocks)


def factor_kernel(
    n_grp, n_pts, chunk, counts, owner, slot_ref, got_ref, high_ref, low_ref, twice_ref, shift_ref,
    out_ref, gain_ref, points, spots,
):
    step = pl.program_id(0)
    rows = out_ref.shape[2]

    @pl.when(step == 0)
    def _():
        group, col = lax.axis_index("grp"), lax.axis_index("pts")
        start = jnp.int32(0)
        for h in range(n_grp):
            count = counts[col, h]
            odd = start & (n_grp - 1)
            begin = lax.div(start, n_grp) + jnp.where(group < odd, 1, 0)
            first = (group - odd) & (n_grp - 1)
            number = jnp.maximum(lax.div(count - first + n_grp - 1, n_grp), 0)

            def move(c, _, h=h, begin=begin):
                at = pl.multiple_of(c * chunk, chunk)
                points[pl.ds(begin + at, chunk), :] = got_ref[h, pl.ds(at, chunk), :].astype(F32)
                return 0

            lax.fori_loop(0, lax.div(number + chunk - 1, chunk), move, 0)
            start += count
        for r in range(ROUNDS):
            own_group, own_col = lax.div(owner[r], n_pts), lax.rem(owner[r], n_pts)
            begin = jnp.int32(0)
            for h in range(n_grp):
                begin += jnp.where(h < own_group, counts[own_col, h], 0)
            rank = begin + slot_ref[r : r + 1, :]
            here = (own_col == col) & ((rank & (n_grp - 1)) == group)
            spots[0:1, r * BLOCK : (r + 1) * BLOCK] = jnp.where(here, rank >> (n_grp.bit_length() - 1), -1)

    base = pl.multiple_of(step * rows, rows)
    wide = points[pl.ds(base, rows), :]
    x = wide.astype(BF16)
    sq = jnp.concatenate(halves(wide * wide), axis=1)
    sq = dot(sq, jnp.ones((2 * EMBED, BLOCK), BF16))
    spot = lax.broadcasted_iota(jnp.int32, (rows, BLOCK), 0) + base
    high, low = [], []
    for r in range(ROUNDS):
        at = slice(r * BLOCK, (r + 1) * BLOCK)
        inner = dot(x, twice_ref[:, at])
        part = jnp.exp2(EXP_SCALE * (inner - sq) + shift_ref[0:1, at])
        part = part + jnp.where(spot == spots[0:1, at], JITTER, 0.0)
        a, b = halves(part)
        high.append(a)
        low.append(b)
    both = 2 * BLOCK
    high01 = jnp.concatenate(high[:2], axis=1)
    low01 = jnp.concatenate(low[:2], axis=1)
    first = (
        dot(high01, high_ref[0:both, :])
        + dot(low01, high_ref[0:both, :])
        + dot(high01, low_ref[0:both, :])
    )
    last = (
        dot(high[2], high_ref[both:, both:])
        + dot(low[2], high_ref[both:, both:])
        + dot(high[2], low_ref[both:, both:])
    )
    parts = [first[:, 0:BLOCK], first[:, BLOCK:both], first[:, both:] + last]
    square = jnp.zeros((rows, BLOCK), F32)
    for r in range(ROUNDS):
        out_ref[0, 0, :, r * BLOCK : (r + 1) * BLOCK] = parts[r].astype(BF16)
        square += parts[r] * parts[r]
    square = jnp.concatenate(halves(square), axis=1)
    gain_ref[...] = (1.0 + JITTER) - dot_nt(jnp.ones((8, 2 * BLOCK), BF16), square)[0:1, :]


def factorize(got, counts, pick_slot, block_owner, high, low, twice, shift, n_grp, n_pts):
    points = got.shape[0] * got.shape[1] // 2
    rows, chunk = 512, 128
    whole = functools.partial(pl.BlockSpec, pipeline_mode=pl.Buffered(1))
    return pl.pallas_call(
        functools.partial(factor_kernel, n_grp, n_pts, chunk),
        grid=(points // rows,),
        out_shape=(
            jax.ShapeDtypeStruct((1, 1, points, FACTOR), BF16),
            jax.ShapeDtypeStruct((1, points), F32),
        ),
        in_specs=[
            pl.BlockSpec(memory_space=pltpu.SMEM),
            pl.BlockSpec(memory_space=pltpu.SMEM),
            whole((ROUNDS, BLOCK), lambda i: (0, 0)),
            whole(got.shape, lambda i: (0, 0, 0)),
            whole((FACTOR, FACTOR), lambda i: (0, 0)),
            whole((FACTOR, FACTOR), lambda i: (0, 0)),
            whole((EMBED, FACTOR), lambda i: (0, 0)),
            whole((1, FACTOR), lambda i: (0, 0)),
        ],
        out_specs=(
            pl.BlockSpec((1, 1, rows, FACTOR), lambda i: (0, 0, i, 0)),
            pl.BlockSpec((1, rows), lambda i: (0, i)),
        ),
        scratch_shapes=[
            pltpu.VMEM((points + chunk, EMBED), F32),
            pltpu.VMEM((1, FACTOR), jnp.int32),
        ],
        compiler_params=pltpu.CompilerParams(vmem_limit_bytes=40 << 20),
        name="factorize",
    )(counts, block_owner, pick_slot, got, high, low, twice, shift)


def per_device(patches, counts, pick_slot, block_owner):
    n_grp, n_pts = lax.axis_size("grp"), lax.axis_size("pts")
    send, picks = pack(patches, counts, pick_slot, block_owner, n_grp, n_pts)
    got = lax.all_to_all(send, "grp", split_axis=0, concat_axis=0, tiled=True)
    blocks = spread(picks, n_grp, n_pts).reshape(FACTOR, EMBED)
    high, low, twice, shift = prepare(blocks)
    rows, gain = factorize(
        got, counts, pick_slot, block_owner, high, low, twice, shift, n_grp, n_pts
    )
    return rows, gain[None]


def solution(mesh):
    in_specs = (P("grp", "pts", None, None), P(), P(), P())
    out_specs = (P("grp", "pts", None, None), P("grp", "pts", None))
    return jax.shard_map(
        per_device, mesh=mesh, in_specs=in_specs, out_specs=out_specs, check_vma=False
    )
```

time: 560 us -> 185 us (0.33)
  waiting for transfers between devices: 284 us -> 0.01 us
  Pallas kernels: 0 us -> 170 us
  local copies, waits for them, and re-layouts: 98.4 us -> 3.51 us
  other arithmetic: 94 us -> 0 us
  matrix products: 51.8 us -> 0 us
  between operations: 17.9 us -> 0.69 us
    psum x1 -> x0, waiting for transfers between devices: 284 us -> none  [from_root(): return lax.psum(block, axis)]
    pallas_call x0 -> x4, Pallas kernels: none -> 170 us  [the longest x1 112 us: spread(): pl.pallas_call(functools.partial(spread_kernel, n_grp, n_pts), out_shape=...]
    gather x4 -> x0, local copies, waits for them, and re-layouts: 87.6 us -> none  [the longest x1 58.2 us: per_device(): jnp.take(local_rows, take_rows, axis=0)]
    another operation x16 -> x0, other arithmetic: 69.9 us -> none  [the longest x9 37.2 us: prepare(): factor_low = jnp.linalg.cholesky(schur_block)]
    dot_general x18 -> x0, matrix products: 50.9 us -> none  [the longest x3 21.4 us: extend(): lax.dot_general(factors, cross_rows, (((1,), (1,)), ((), ())), precision=...]
    select_n x7 -> x0, other arithmetic: 9.18 us -> none  [the longest x1 7.62 us: per_device(): jnp.where(keep_mask, shaped, jnp.zeros((), local_rows.dtype))]
    concatenate x5 -> x0, other arithmetic: 7.71 us -> none  [the longest x4 7.69 us: extend(): return jnp.concatenate([factors, fresh_rows], axis=1)]
  transfers between devices with their start and end apart: 2 -> 1, of which waited for: 1 -> 0; matrix products, arithmetic and copies ran while one was open for 15% -> 0% of each run, Pallas kernels for 0% -> 75%
where the time goes in v1:
time: 185 us; the launch traced here: 184 us
  Pallas kernels  170 us (92%)
  starting transfers between devices  9.98 us (5%)
  local copies, waits for them, and re-layouts  3.51 us (2%)
    pallas_call x1, Pallas kernels, spread(): pl.pallas_call(functools.partial(spread_kernel, n_grp, n_pts), out_shape=...  112 us
    pallas_call x1, Pallas kernels, prepare(): pl.pallas_call(prepare_kernel, out_shape=(jax.ShapeDtypeStruct((FACTOR, F...  25.7 us
    pallas_call x1, Pallas kernels, factorize(): pl.pallas_call(functools.partial(factor_kernel, n_grp, n_pts, chunk), gri...  23.1 us
    all_to_all x1, starting transfers between devices, per_device(): got = lax.all_to_all(send, 'grp', split_axis=0, concat_axis=0, tiled=True)  9.98 us
    pallas_call x1, Pallas kernels, pack(): pl.pallas_call(functools.partial(pack_kernel, n_grp, n_pts), grid=(steps,...  8.94 us
  transfers between devices with their start and end apart: 1, of which 0 were waited for; matrix products, arithmetic and copies ran while one was open for 0% of the time, Pallas kernels for 75%

profile of v1, /device:TPU:1, one launch (start us, length us, event | category | flops | bytes accessed | tf_op | source)
XLA Modules:
  0.0 184.3 jit_solution(6282528940130556853)
XLA Ops:
  0.6 8.9 %pack.1 = (bf16[16,1024,128]{2,1,0:T(8,128)(2,1)}, bf16[3,128,128]{2,1,0:T(8,128)(2,1)}) custom-call(s32[16,16]{1,0:T(8,128)} %counts.3, s32[3]{0:T(128)} %owner.3, s32[3,128]{1,0:T(4,128)} %slot_ref.3, bf16[1,1,16384,128]{3,2,1,0:T(8,128)(2,1)} %x_ref.1), custom_call_target="tpu_custom_call" | custom-call | tf_op jit(solution)/shard_map/pack/pallas_call | solution.py:84
  9.6 10.0 %all-to-all-start = ((bf16[16,1024,128]{2,1,0:T(8,128)(2,1)}), bf16[16,1024,128]{2,1,0:T(8,128)(2,1)}, u32[]{:S(2)}, u32[]{:S(2)}) async-start(bf16[16,1024,128]{2,1,0:T(8,128)(2,1)} %get-tuple-element.10), calls=%async_computation | async-start | bytes 8388608 | tf_op jit(solution)/shard_map/all_to_all | solution.py:445
  19.6 112.3 %spread.1 = bf16[12,32,128]{2,1,0:T(8,128)(2,1)} custom-call(bf16[12,32,128]{2,1,0:T(8,128)(2,1)} %bitcast.3), custom_call_target="tpu_custom_call" | custom-call | flops 20000000000 | bytes 200000 | tf_op jit(solution)/shard_map/spread/pallas_call | solution.py:208
  131.9 0.0 copy-start.3
  131.9 0.0 copy-start.4
  131.9 0.0 copy-start.5
  131.9 25.7 %prepare.1 = (bf16[384,384]{1,0:T(8,128)(2,1)}, bf16[384,384]{1,0:T(8,128)(2,1)}, bf16[128,384]{1,0:T(8,128)(2,1)}, f32[1,384]{1,0:T(1,128)}) custom-call(bf16[384,128]{1,0:T(8,128)(2,1)} %bitcast.5), custom_call_target="tpu_custom_call" | custom-call | flops 40000000000 | bytes 900000 | tf_op jit(solution)/shard_map/prepare/pallas_call | solution.py:317
  157.6 0.0 all-to-all-done.got_ref
  157.6 0.0 copy-done.3
  157.6 0.0 copy-done.4
  157.7 0.0 copy-done.5
  157.7 0.0 copy-start
  157.7 1.0 copy-done
  158.6 0.0 copy-start.1
  158.6 1.0 copy-done.1
  159.6 0.0 copy-start.2
  159.6 0.9 copy-done.2
  160.5 0.0 copy-start.6
  160.5 0.7 copy-done.6
  161.2 23.1 %factorize.1 = (bf16[1,1,8192,384]{3,2,1,0:T(8,128)(2,1)}, f32[1,8192]{1,0:T(1,128)}) custom-call(s32[16,16]{1,0:T(8,128)S(1)} %copy-done.3, s32[3]{0:T(128)S(1)} %copy-done.5, s32[3,128]{1,0:T(4,128)S(1)} %copy-done.4, bf16[16,1024,128]{2,1,0:T(8,128)(2,1)} %all-to-all-done.got_ref, bf16[384,384]{1,0:T(8,128)(2,1)S(1)} %copy-done, ...), custom_call_target="tpu_custom_call" | custom-call | tf_op jit(solution)/shard_map/factorize/pallas_call | solution.py:412
Async XLA Ops:
  9.6 148.1 %all-to-all-start = ((bf16[16,1024,128]{2,1,0:T(8,128)(2,1)}), bf16[16,1024,128]{2,1,0:T(8,128)(2,1)}, u32[]{:S(2)}, u32[]{:S(2)}) async-start(bf16[16,1024,128]{2,1,0:T(8,128)(2,1)} %get-tuple-element.10), calls=%async_computation | async-start | bytes 8388608 | tf_op jit(solution)/shard_map/all_to_all | solution.py:445
  131.9 25.8 %copy-start.3 = (s32[16,16]{1,0:T(8,128)S(1)}, s32[16,16]{1,0:T(8,128)}, u32[]{:S(2)}) copy-start(s32[16,16]{1,0:T(8,128)} %counts.3) | copy-start | bytes 3076
  131.9 25.8 %copy-start.4 = (s32[3,128]{1,0:T(4,128)S(1)}, s32[3,128]{1,0:T(4,128)}, u32[]{:S(2)}) copy-start(s32[3,128]{1,0:T(4,128)} %slot_ref.3) | copy-start | bytes 4612
  131.9 25.8 %copy-start.5 = (s32[3]{0:T(128)S(1)}, s32[3]{0:T(128)}, u32[]{:S(2)}) copy-start(s32[3]{0:T(128)} %owner.3) | copy-start | bytes 40
  157.7 1.0 copy-start
  158.6 1.0 copy-start.1
  159.6 0.9 copy-start.2
  160.5 0.7 copy-start.6

commit v2 on v1

--- a/solution.py
+++ b/solution.py
@@ -17,6 +17,7 @@
 FACTOR = ROUNDS * BLOCK
 PARTS = 12
 PART_ROWS = FACTOR // PARTS
+FIRST_ROWS = 128
 EXP_SCALE = math.log2(math.e) / EMBED
 F32 = jnp.float32
 BF16 = jnp.bfloat16
@@ -37,18 +38,27 @@
     return high, (x - high.astype(F32)).astype(BF16)
 
 
-def pack_kernel(n_grp, n_pts, counts, owner, slot_ref, x_ref, out_ref, picks_ref, wide, column, total):
+def pack_kernel(n_grp, n_pts, counts, owner, slot_ref, x_ref, out_ref, picks_ref, order, column, total):
     step = pl.program_id(0)
     group, col = lax.axis_index("grp"), lax.axis_index("pts")
     me = group * n_pts + col
-    rows = wide.shape[0]
-    start = jnp.int32(0)
-    for h in range(n_grp):
-        start += jnp.where(h < group, counts[col, h], 0)
-    wide[...] = x_ref[0, 0].astype(F32)
-    for t in range(n_grp):
-        first = (t - start) & (n_grp - 1)
-        out_ref[t] = wide[pl.ds(first, rows // n_grp, stride=n_grp), :].astype(BF16)
+    rows = x_ref.shape[2]
+    tile = order.shape[0]
+    each = tile // n_grp
+
+    @pl.when(step == 0)
+    def _():
+        start = jnp.int32(0)
+        for h in range(n_grp):
+            start += jnp.where(h < group, counts[col, h], 0)
+        to = lax.broadcasted_iota(jnp.int32, (tile, tile), 0)
+        source = (to & (each - 1)) * n_grp + (((to >> (each.bit_length() - 1)) - start) & (n_grp - 1))
+        hit = source == lax.broadcasted_iota(jnp.int32, (tile, tile), 1)
+        order[...] = hit.astype(F32).astype(BF16)
+
+    for c in range(rows // tile):
+        moved = dot(order[...], x_ref[0, 0, c * tile : (c + 1) * tile, :]).astype(BF16)
+        out_ref[:, c * each : (c + 1) * each, :] = moved.reshape(n_grp, each, EMBED)
 
     mine = (owner[0] == me) | (owner[1] == me) | (owner[2] == me)
 
@@ -99,7 +109,7 @@
             pl.BlockSpec((ROUNDS, BLOCK, EMBED), lambda i: (0, 0, 0)),
         ),
         scratch_shapes=[
-            pltpu.VMEM((rows, EMBED), F32),
+            pltpu.VMEM((n_grp * 16, n_grp * 16), BF16),
             pltpu.VMEM((BLOCK, BLOCK), jnp.int32),
             pltpu.VMEM((BLOCK, EMBED), F32),
         ],
@@ -107,120 +117,25 @@
     )(counts, block_owner, pick_slot, patches)
 
 
-def spread_kernel(n_grp, n_pts, in_ref, out_ref, got1, got2, part, gathered, s1, r1, s2, r2, s3, r3):
+def greet(axis_sizes, place):
+    barrier = pltpu.get_barrier_semaphore()
+    total = 0
+    for axis, size in axis_sizes:
+        for d in range(1, size):
+            pl.semaphore_signal(barrier, inc=1, device_id=place(axis, d), device_id_type=MESH)
+        total += size - 1
+    pl.semaphore_wait(barrier, total)
+
+
+def neighbour(n_grp, n_pts):
     group, col = lax.axis_index("grp"), lax.axis_index("pts")
-    barrier = pltpu.get_barrier_semaphore()
-    for d in range(1, n_grp):
-        pl.semaphore_signal(
-            barrier, inc=1, device_id=(lax.rem(group + d, n_grp), col), device_id_type=MESH
-        )
-    for d in range(1, n_pts):
-        pl.semaphore_signal(
-            barrier, inc=1, device_id=(group, lax.rem(col + d, n_pts)), device_id_type=MESH
-        )
-    pl.semaphore_wait(barrier, n_grp + n_pts - 2)
-
-    def scatter(d):
-        target = lax.rem(group + d, n_grp)
-        source = jnp.minimum(target, PARTS - 1)
-        return target, pltpu.make_async_remote_copy(
-            src_ref=in_ref.at[source],
-            dst_ref=got1.at[d - 1],
-            send_sem=s1.at[d],
-            recv_sem=r1.at[d],
-            device_id=(target, col),
-            device_id_type=MESH,
-        )
-
-    def across(d):
-        return pltpu.make_async_remote_copy(
-            src_ref=part.at[0],
-            dst_ref=got2.at[d - 1],
-            send_sem=s2.at[d],
-            recv_sem=r2.at[d],
-            device_id=(group, lax.rem(col + d, n_pts)),
-            device_id_type=MESH,
-        )
-
-    def gather(d, owner):
-        return pltpu.make_async_remote_copy(
-            src_ref=part.at[1],
-            dst_ref=gathered.at[owner],
-            send_sem=s3.at[d],
-            recv_sem=r3.at[d],
-            device_id=(lax.rem(group + d, n_grp), col),
-            device_id_type=MESH,
-        )
-
-    for d in range(1, n_grp):
-        target, copy = scatter(d)
-
-        @pl.when(target < PARTS)
-        def _():
-            copy.start()
-
-    @pl.when(group < PARTS)
-    def _():
-        for d in range(1, n_grp):
-            scatter(d)[1].wait_recv()
-        acc = in_ref[jnp.minimum(group, PARTS - 1)].astype(F32)
-        for d in range(1, n_grp):
-            acc += got1[d - 1].astype(F32)
-        part[0] = acc.astype(BF16)
-        for d in range(1, n_pts):
-            across(d).start()
-        for d in range(1, n_pts):
-            across(d).wait_recv()
-        acc = part[0].astype(F32)
-        for d in range(1, n_pts):
-            acc += got2[d - 1].astype(F32)
-        part[1] = acc.astype(BF16)
-        for d in range(1, n_grp):
-            gather(d, group).start()
-        gathered[group] = part[1]
-
-    for d in range(1, n_grp):
-        source = lax.rem(group + n_grp - d, n_grp)
-
-        @pl.when(source < PARTS)
-        def _():
-            gather(d, source).wait_recv()
-
-    out_ref[...] = gathered[...]
-
-    for d in range(1, n_grp):
-        target, copy = scatter(d)
-
-        @pl.when(target < PARTS)
-        def _():
-            copy.wait_send()
-
-    @pl.when(group < PARTS)
-    def _():
-        for d in range(1, n_pts):
-            across(d).wait_send()
-        for d in range(1, n_grp):
-            gather(d, group).wait_send()
-
-
-def spread(picks, n_grp, n_pts):
-    shape = (PARTS, PART_ROWS, EMBED)
-    return pl.pallas_call(
-        functools.partial(spread_kernel, n_grp, n_pts),
-        out_shape=jax.ShapeDtypeStruct(shape, BF16),
-        in_specs=[pl.BlockSpec(memory_space=pltpu.VMEM)],
-        out_specs=pl.BlockSpec(memory_space=pltpu.VMEM),
-        scratch_shapes=[
-            pltpu.VMEM((n_grp - 1,) + shape[1:], BF16),
-            pltpu.VMEM((n_pts - 1,) + shape[1:], BF16),
-            pltpu.VMEM((2,) + shape[1:], BF16),
-            pltpu.VMEM(shape, BF16),
-        ]
-        + [pltpu.SemaphoreType.DMA((max(n_grp, n_pts),))] * 6,
-        compiler_params=pltpu.CompilerParams(collective_id=0, has_side_effects=True),
-        cost_estimate=pl.CostEstimate(flops=20_000_000_000, bytes_accessed=200_000, transcendentals=0),
-        name="spread",
-    )(picks.reshape(shape))
+
+    def place(axis, d):
+        if axis == "grp":
+            return (lax.rem(group + d, n_grp), col)
+        return (group, lax.rem(col + d, n_pts))
+
+    return place
 
 
 def unit_inverse(a_ref, m_ref):
@@ -260,16 +175,14 @@
         m_ref[low : low + 8, :] = pm * scale
 
 
-def prepare_kernel(b_ref, high_ref, low_ref, twice_ref, shift_ref, schur, work, inv):
-    blocks = b_ref[...]
+def prepare(blocks, weights_ref, schur, work, inv):
     wide = blocks.astype(F32)
     sq_high, sq_low = halves(wide * wide)
     ones = jnp.ones((EMBED, BLOCK), BF16)
     sq_col = dot(sq_high, ones) + dot(sq_low, ones)
     row_ones = jnp.ones((8, EMBED), BF16)
     sq_row = (dot_nt(row_ones, sq_high) + dot_nt(row_ones, sq_low))[0:1, :]
-    shift_ref[...] = -EXP_SCALE * sq_row
-    twice_ref[...] = (2.0 * wide).T.astype(BF16)
+    weights_ref[2 * FACTOR :, :] = (2.0 * wide).T.astype(BF16)
     eye = (
         lax.broadcasted_iota(jnp.int32, (BLOCK, BLOCK), 0)
         == lax.broadcasted_iota(jnp.int32, (BLOCK, BLOCK), 1)
@@ -308,35 +221,163 @@
                 high, low = halves(inv[i, j].T)
             else:
                 high = low = jnp.zeros((BLOCK, BLOCK), BF16)
-            high_ref[span(j), span(i)] = high
-            low_ref[span(j), span(i)] = low
-
-
-def prepare(blocks):
+            weights_ref[span(j), span(i)] = high
+            weights_ref[span(ROUNDS + j), span(i)] = low
+
+
+def exchange_kernel(
+    n_grp, n_pts, send_ref, picks_ref, got_ref, weights_ref,
+    got1, got2, part, gathered, schur, work, inv, own_sem, *sems,
+):
+    group, col = lax.axis_index("grp"), lax.axis_index("pts")
+    place = neighbour(n_grp, n_pts)
+    greet((("pts", n_pts), ("grp", n_grp)), place)
+    (s1, r1), (s2, r2), (s3, r3) = sems[0:2], sems[2:4], sems[4:6]
+    bulk = sems[6:]
+    edges = (0, FIRST_ROWS, send_ref.shape[1])
+    order = sorted(range(1, n_grp), key=lambda d: -min(d, n_grp - d))
+
+    def rows(piece, d):
+        span = pl.ds(edges[piece], edges[piece + 1] - edges[piece])
+        target = lax.rem(group + d, n_grp)
+        return pltpu.make_async_remote_copy(
+            src_ref=send_ref.at[target, span],
+            dst_ref=got_ref.at[group, span],
+            send_sem=bulk[2 * piece].at[d],
+            recv_sem=bulk[2 * piece + 1].at[d],
+            device_id=place("grp", d),
+            device_id_type=MESH,
+        )
+
+    def scatter(d):
+        target = lax.rem(col + d, n_pts)
+        return target, pltpu.make_async_remote_copy(
+            src_ref=picks_ref.at[jnp.minimum(target, PARTS - 1)],
+            dst_ref=got1.at[d - 1],
+            send_sem=s1.at[d],
+            recv_sem=r1.at[d],
+            device_id=place("pts", d),
+            device_id_type=MESH,
+        )
+
+    def across(d):
+        return pltpu.make_async_remote_copy(
+            src_ref=part.at[0],
+            dst_ref=got2.at[d - 1],
+            send_sem=s2.at[d],
+            recv_sem=r2.at[d],
+            device_id=place("grp", d),
+            device_id_type=MESH,
+        )
+
+    def gather(d, owner):
+        return pltpu.make_async_remote_copy(
+            src_ref=part.at[1],
+            dst_ref=gathered.at[owner],
+            send_sem=s3.at[d],
+            recv_sem=r3.at[d],
+            device_id=place("pts", d),
+            device_id_type=MESH,
+        )
+
+    for d in range(1, n_pts):
+        target, copy = scatter(d)
+
+        @pl.when(target < PARTS)
+        def _():
+            copy.start()
+
+    own = pltpu.make_async_copy(send_ref.at[group], got_ref.at[group], own_sem)
+    own.start()
+    for d in order:
+        rows(0, d).start()
+
+    @pl.when(col < PARTS)
+    def _():
+        acc = picks_ref[jnp.minimum(col, PARTS - 1)].astype(F32)
+        for d in range(1, n_pts):
+            scatter(d)[1].wait_recv()
+            acc += got1[d - 1].astype(F32)
+        part[0] = acc.astype(BF16)
+        for d in range(1, n_grp):
+            across(d).start()
+
+    for d in order:
+        rows(1, d).start()
+
+    @pl.when(col < PARTS)
+    def _():
+        acc = part[0].astype(F32)
+        for d in range(1, n_grp):
+            across(d).wait_recv()
+            acc += got2[d - 1].astype(F32)
+        part[1] = acc.astype(BF16)
+        for d in range(1, n_pts):
+            gather(d, col).start()
+        gathered[col] = part[1]
+
+    for d in range(1, n_pts):
+        source = lax.rem(col + n_pts - d, n_pts)
+
+        @pl.when(source < PARTS)
+        def _():
+            gather(d, source).wait_recv()
+
+    prepare(gathered[...].reshape(FACTOR, EMBED), weights_ref, schur, work, inv)
+
+    for d in range(1, n_pts):
+        target, copy = scatter(d)
+
+        @pl.when(target < PARTS)
+        def _():
+            copy.wait_send()
+
+    @pl.when(col < PARTS)
+    def _():
+        for d in range(1, n_grp):
+            across(d).wait_send()
+        for d in range(1, n_pts):
+            gather(d, col).wait_send()
+
+    own.wait()
+    for piece in range(2):
+        for d in order:
+            rows(piece, d).wait()
+
+
+def exchange(send, picks, n_grp, n_pts):
+    shape = (PARTS, PART_ROWS, EMBED)
     square = (ROUNDS, ROUNDS, BLOCK, BLOCK)
     return pl.pallas_call(
-        prepare_kernel,
+        functools.partial(exchange_kernel, n_grp, n_pts),
         out_shape=(
-            jax.ShapeDtypeStruct((FACTOR, FACTOR), BF16),
-            jax.ShapeDtypeStruct((FACTOR, FACTOR), BF16),
-            jax.ShapeDtypeStruct((EMBED, FACTOR), BF16),
-            jax.ShapeDtypeStruct((1, FACTOR), F32),
+            jax.ShapeDtypeStruct(send.shape, BF16),
+            jax.ShapeDtypeStruct((2 * FACTOR + EMBED, FACTOR), BF16),
         ),
-        in_specs=[pl.BlockSpec(memory_space=pltpu.VMEM)],
-        out_specs=(pl.BlockSpec(memory_space=pltpu.VMEM),) * 4,
+        in_specs=[pl.BlockSpec(memory_space=pltpu.HBM), pl.BlockSpec(memory_space=pltpu.VMEM)],
+        out_specs=(pl.BlockSpec(memory_space=pltpu.HBM), pl.BlockSpec(memory_space=pltpu.VMEM)),
         scratch_shapes=[
+            pltpu.VMEM((n_pts - 1,) + shape[1:], BF16),
+            pltpu.VMEM((n_grp - 1,) + shape[1:], BF16),
+            pltpu.VMEM((2,) + shape[1:], BF16),
+            pltpu.VMEM(shape, BF16),
             pltpu.VMEM(square, F32),
             pltpu.VMEM((BLOCK, BLOCK), F32),
             pltpu.VMEM(square, F32),
-        ],
-        cost_estimate=pl.CostEstimate(flops=40_000_000_000, bytes_accessed=900_000, transcendentals=0),
-        name="prepare",
-    )(blocks)
+            pltpu.SemaphoreType.DMA,
+        ]
+        + [pltpu.SemaphoreType.DMA((n,)) for n in (n_pts, n_pts, n_grp, n_grp, n_pts, n_pts)]
+        + [pltpu.SemaphoreType.DMA((n_grp,))] * 4,
+        compiler_params=pltpu.CompilerParams(
+            collective_id=0, has_side_effects=True, vmem_limit_bytes=24 << 20
+        ),
+        name="exchange",
+    )(send, picks.reshape(shape))
 
 
 def factor_kernel(
-    n_grp, n_pts, chunk, counts, owner, slot_ref, got_ref, high_ref, low_ref, twice_ref, shift_ref,
-    out_ref, gain_ref, points, spots,
+    n_grp, n_pts, chunk, counts, owner, slot_ref, got_ref, weights_ref,
+    out_ref, gain_ref, points, spots, shift_ref,
 ):
     step = pl.program_id(0)
     rows = out_ref.shape[2]
@@ -368,6 +409,13 @@
             here = (own_col == col) & ((rank & (n_grp - 1)) == group)
             spots[0:1, r * BLOCK : (r + 1) * BLOCK] = jnp.where(here, rank >> (n_grp.bit_length() - 1), -1)
 
+        twice = weights_ref[2 * FACTOR :, :].astype(F32)
+        twice_high, twice_low = halves(twice * twice)
+        ones = jnp.ones((8, EMBED), BF16)
+        shift_ref[...] = (-0.25 * EXP_SCALE) * (dot(ones, twice_high) + dot(ones, twice_low))[0:1, :]
+
+    high_ref, low_ref = weights_ref.at[0:FACTOR], weights_ref.at[FACTOR : 2 * FACTOR]
+    twice_ref = weights_ref.at[2 * FACTOR :]
     base = pl.multiple_of(step * rows, rows)
     wide = points[pl.ds(base, rows), :]
     x = wide.astype(BF16)
@@ -405,7 +453,7 @@
     gain_ref[...] = (1.0 + JITTER) - dot_nt(jnp.ones((8, 2 * BLOCK), BF16), square)[0:1, :]
 
 
-def factorize(got, counts, pick_slot, block_owner, high, low, twice, shift, n_grp, n_pts):
+def factorize(got, counts, pick_slot, block_owner, weights, n_grp, n_pts):
     points = got.shape[0] * got.shape[1] // 2
     rows, chunk = 512, 128
     whole = functools.partial(pl.BlockSpec, pipeline_mode=pl.Buffered(1))
@@ -421,10 +469,7 @@
             pl.BlockSpec(memory_space=pltpu.SMEM),
             whole((ROUNDS, BLOCK), lambda i: (0, 0)),
             whole(got.shape, lambda i: (0, 0, 0)),
-            whole((FACTOR, FACTOR), lambda i: (0, 0)),
-            whole((FACTOR, FACTOR), lambda i: (0, 0)),
-            whole((EMBED, FACTOR), lambda i: (0, 0)),
-            whole((1, FACTOR), lambda i: (0, 0)),
+            whole(weights.shape, lambda i: (0, 0)),
         ],
         out_specs=(
             pl.BlockSpec((1, 1, rows, FACTOR), lambda i: (0, 0, i, 0)),
@@ -433,21 +478,18 @@
         scratch_shapes=[
             pltpu.VMEM((points + chunk, EMBED), F32),
             pltpu.VMEM((1, FACTOR), jnp.int32),
+            pltpu.VMEM((1, FACTOR), F32),
         ],
         compiler_params=pltpu.CompilerParams(vmem_limit_bytes=40 << 20),
         name="factorize",
-    )(counts, block_owner, pick_slot, got, high, low, twice, shift)
+    )(counts, block_owner, pick_slot, got, weights)
 
 
 def per_device(patches, counts, pick_slot, block_owner):
     n_grp, n_pts = lax.axis_size("grp"), lax.axis_size("pts")
     send, picks = pack(patches, counts, pick_slot, block_owner, n_grp, n_pts)
-    got = lax.all_to_all(send, "grp", split_axis=0, concat_axis=0, tiled=True)
-    blocks = spread(picks, n_grp, n_pts).reshape(FACTOR, EMBED)
-    high, low, twice, shift = prepare(blocks)
-    rows, gain = factorize(
-        got, counts, pick_slot, block_owner, high, low, twice, shift, n_grp, n_pts
-    )
+    got, weights = exchange(send, picks, n_grp, n_pts)
+    rows, gain = factorize(got, counts, pick_slot, block_owner, weights, n_grp, n_pts)
     return rows, gain[None]
 
 

time: 185 us -> 140 us (0.76)
  Pallas kernels: 170 us -> 135 us
  starting transfers between devices: 9.98 us -> 0 us
    pallas_call x2 -> x1, Pallas kernels: 138 us -> 105 us  [exchange(): pl.pallas_call(functools.partial(exchange_kernel, n_grp, n_pts), out_shap...]
    all_to_all x1 -> x0, starting transfers between devices: 9.98 us -> none  [per_device(): got = lax.all_to_all(send, 'grp', split_axis=0, concat_axis=0, tiled=True)]
  transfers between devices with their start and end apart: 1 -> 0, of which waited for: 0 -> 0; matrix products, arithmetic and copies ran while one was open for 0% -> 0% of each run, Pallas kernels for 75% -> 0%
where the time goes in v2:
time: 140 us; the launch traced here: 138 us
  Pallas kernels  135 us (96%)
  local copies, waits for them, and re-layouts  3.09 us (2%)
    pallas_call x1, Pallas kernels, exchange(): pl.pallas_call(functools.partial(exchange_kernel, n_grp, n_pts), out_shap...  105 us
    pallas_call x1, Pallas kernels, factorize(): pl.pallas_call(functools.partial(factor_kernel, n_grp, n_pts, chunk), gri...  21.9 us
    pallas_call x1, Pallas kernels, pack(): pl.pallas_call(functools.partial(pack_kernel, n_grp, n_pts), grid=(steps,...  8.19 us
    unnamed x10, local copies, waits for them, and re-layouts  3.09 us

profile of v2, /device:TPU:1, one launch (start us, length us, event | category | flops | bytes accessed | tf_op | source)
XLA Modules:
  0.0 138.5 jit_solution(18174542160146150199)
XLA Ops:
  0.6 0.0 copy-start.4
  0.6 0.0 copy-start.3
  0.7 0.0 copy-start.2
  0.7 8.2 %pack.1 = (bf16[16,1024,128]{2,1,0:T(8,128)(2,1)}, bf16[3,128,128]{2,1,0:T(8,128)(2,1)}) custom-call(s32[16,16]{1,0:T(8,128)} %counts.3, s32[3]{0:T(128)} %owner.3, s32[3,128]{1,0:T(4,128)} %slot_ref.3, bf16[1,1,16384,128]{3,2,1,0:T(8,128)(2,1)} %x_ref.1), custom_call_target="tpu_custom_call" | custom-call | tf_op jit(solution)/shard_map/pack/pallas_call | solution.py:94
  8.8 0.0 copy-start
  8.8 2.2 %copy-done = bf16[16,1024,128]{2,1,0:T(8,128)(2,1)S(1)} copy-done((bf16[16,1024,128]{2,1,0:T(8,128)(2,1)S(1)}, bf16[16,1024,128]{2,1,0:T(8,128)(2,1)}, u32[]{:S(2)}) %copy-start) | copy-done | bytes 4194328
  11.0 0.0 copy-start.1
  11.0 0.9 copy-done.1
  11.9 104.6 %exchange.1 = (bf16[16,1024,128]{2,1,0:T(8,128)(2,1)S(1)}, bf16[896,384]{1,0:T(8,128)(2,1)S(1)}) custom-call(bf16[16,1024,128]{2,1,0:T(8,128)(2,1)S(1)} %copy-done, bf16[12,32,128]{2,1,0:T(8,128)(2,1)S(1)} %bitcast.2), custom_call_target="tpu_custom_call" | custom-call | tf_op jit(solution)/shard_map/exchange/pallas_call | solution.py:351
  116.6 0.0 copy-done.4
  116.6 0.0 copy-done.3
  116.6 0.0 copy-done.2
  116.6 21.9 %factorize.1 = (bf16[1,1,8192,384]{3,2,1,0:T(8,128)(2,1)}, f32[1,8192]{1,0:T(1,128)}) custom-call(s32[16,16]{1,0:T(8,128)S(1)} %copy-done.2, s32[3]{0:T(128)S(1)} %copy-done.4, s32[3,128]{1,0:T(4,128)S(1)} %copy-done.3, bf16[16,1024,128]{2,1,0:T(8,128)(2,1)S(1)} %get-tuple-element.10.got_ref, bf16[896,384]{1,0:T(8,128)(2,1)S(1)} %get-tuple-element.11.weights_ref), custom_call_target="tpu_custom_call" | custom-call | tf_op jit(solution)/shard_map/factorize/pallas_call | solution.py:460
Async XLA Ops:
  0.6 115.9 %copy-start.4 = (s32[3]{0:T(128)S(1)}, s32[3]{0:T(128)}, u32[]{:S(2)}) copy-start(s32[3]{0:T(128)} %owner.3) | copy-start | bytes 40
  0.6 115.9 %copy-start.3 = (s32[3,128]{1,0:T(4,128)S(1)}, s32[3,128]{1,0:T(4,128)}, u32[]{:S(2)}) copy-start(s32[3,128]{1,0:T(4,128)} %slot_ref.3) | copy-start | bytes 4612
  0.7 115.9 %copy-start.2 = (s32[16,16]{1,0:T(8,128)S(1)}, s32[16,16]{1,0:T(8,128)}, u32[]{:S(2)}) copy-start(s32[16,16]{1,0:T(8,128)} %counts.3) | copy-start | bytes 3076
  8.8 2.2 %copy-start = (bf16[16,1024,128]{2,1,0:T(8,128)(2,1)S(1)}, bf16[16,1024,128]{2,1,0:T(8,128)(2,1)}, u32[]{:S(2)}) copy-start(bf16[16,1024,128]{2,1,0:T(8,128)(2,1)} %get-tuple-element.8.send_ref) | copy-start | bytes 12582916
  11.0 0.9 copy-start.1

commit v3 on v2

--- a/solution.py
+++ b/solution.py
@@ -17,7 +17,7 @@
 FACTOR = ROUNDS * BLOCK
 PARTS = 12
 PART_ROWS = FACTOR // PARTS
-FIRST_ROWS = 128
+FIRST_ROWS = 256
 EXP_SCALE = math.log2(math.e) / EMBED
 F32 = jnp.float32
 BF16 = jnp.bfloat16
@@ -38,92 +38,14 @@
     return high, (x - high.astype(F32)).astype(BF16)
 
 
-def pack_kernel(n_grp, n_pts, counts, owner, slot_ref, x_ref, out_ref, picks_ref, order, column, total):
-    step = pl.program_id(0)
-    group, col = lax.axis_index("grp"), lax.axis_index("pts")
-    me = group * n_pts + col
-    rows = x_ref.shape[2]
-    tile = order.shape[0]
-    each = tile // n_grp
-
-    @pl.when(step == 0)
-    def _():
-        start = jnp.int32(0)
-        for h in range(n_grp):
-            start += jnp.where(h < group, counts[col, h], 0)
-        to = lax.broadcasted_iota(jnp.int32, (tile, tile), 0)
-        source = (to & (each - 1)) * n_grp + (((to >> (each.bit_length() - 1)) - start) & (n_grp - 1))
-        hit = source == lax.broadcasted_iota(jnp.int32, (tile, tile), 1)
-        order[...] = hit.astype(F32).astype(BF16)
-
-    for c in range(rows // tile):
-        moved = dot(order[...], x_ref[0, 0, c * tile : (c + 1) * tile, :]).astype(BF16)
-        out_ref[:, c * each : (c + 1) * each, :] = moved.reshape(n_grp, each, EMBED)
-
-    mine = (owner[0] == me) | (owner[1] == me) | (owner[2] == me)
-
-    @pl.when(step == 0)
-    def _():
-        total[...] = jnp.zeros_like(total)
-        for r in range(ROUNDS):
-
-            @pl.when(owner[r] == me)
-            def _():
-                column[...] = jnp.broadcast_to(slot_ref[r : r + 1, :], (BLOCK, BLOCK)).T
-
-    @pl.when(mine)
-    def _():
-        lane = lax.broadcasted_iota(jnp.int32, (BLOCK, BLOCK), 1)
-        wanted = column[...] - step * rows
-        acc = total[...]
-        for c in range(rows // BLOCK):
-            hit = (wanted == lane + c * BLOCK).astype(F32).astype(BF16)
-            acc += dot(hit, x_ref[0, 0, c * BLOCK : (c + 1) * BLOCK, :])
-        total[...] = acc
-
-    @pl.when(step == pl.num_programs(0) - 1)
-    def _():
-        for r in range(ROUNDS):
-            picks_ref[r] = jnp.where(owner[r] == me, total[...], 0.0).astype(BF16)
-
-
-def pack(patches, counts, pick_slot, block_owner, n_grp, n_pts):
-    slots = patches.shape[2]
-    steps = 8
-    rows = slots // steps
-    return pl.pallas_call(
-        functools.partial(pack_kernel, n_grp, n_pts),
-        grid=(steps,),
-        out_shape=(
-            jax.ShapeDtypeStruct((n_grp, slots // n_grp, EMBED), BF16),
-            jax.ShapeDtypeStruct((ROUNDS, BLOCK, EMBED), BF16),
-        ),
-        in_specs=[
-            pl.BlockSpec(memory_space=pltpu.SMEM),
-            pl.BlockSpec(memory_space=pltpu.SMEM),
-            pl.BlockSpec((ROUNDS, BLOCK), lambda i: (0, 0)),
-            pl.BlockSpec((1, 1, rows, EMBED), lambda i: (0, 0, i, 0)),
-        ],
-        out_specs=(
-            pl.BlockSpec((n_grp, rows // n_grp, EMBED), lambda i: (0, i, 0)),
-            pl.BlockSpec((ROUNDS, BLOCK, EMBED), lambda i: (0, 0, 0)),
-        ),
-        scratch_shapes=[
-            pltpu.VMEM((n_grp * 16, n_grp * 16), BF16),
-            pltpu.VMEM((BLOCK, BLOCK), jnp.int32),
-            pltpu.VMEM((BLOCK, EMBED), F32),
-        ],
-        name="pack",
-    )(counts, block_owner, pick_slot, patches)
-
-
-def greet(axis_sizes, place):
+def greet(axis_sizes, place, meanwhile):
     barrier = pltpu.get_barrier_semaphore()
     total = 0
     for axis, size in axis_sizes:
         for d in range(1, size):
             pl.semaphore_signal(barrier, inc=1, device_id=place(axis, d), device_id_type=MESH)
         total += size - 1
+    meanwhile()
     pl.semaphore_wait(barrier, total)
 
 
@@ -226,16 +148,66 @@
 
 
 def exchange_kernel(
-    n_grp, n_pts, send_ref, picks_ref, got_ref, weights_ref,
-    got1, got2, part, gathered, schur, work, inv, own_sem, *sems,
+    n_grp, n_pts, counts, owner, slot_ref, patches_ref, got_ref, weights_ref,
+    x_ref, send_ref, order, picks_ref, got1, got2, part, gathered, schur, work, inv,
+    load_sems, own_sem, *sems,
 ):
     group, col = lax.axis_index("grp"), lax.axis_index("pts")
+    me = group * n_pts + col
     place = neighbour(n_grp, n_pts)
-    greet((("pts", n_pts), ("grp", n_grp)), place)
     (s1, r1), (s2, r2), (s3, r3) = sems[0:2], sems[2:4], sems[4:6]
     bulk = sems[6:]
-    edges = (0, FIRST_ROWS, send_ref.shape[1])
-    order = sorted(range(1, n_grp), key=lambda d: -min(d, n_grp - d))
+    per_peer = send_ref.shape[1]
+    edges = (0, FIRST_ROWS, per_peer)
+    tile = order.shape[0]
+    each = tile // n_grp
+    loads = load_sems.shape[0]
+    load_rows = x_ref.shape[0] // loads
+    far_first = sorted(range(1, n_grp), key=lambda d: -min(d, n_grp - d))
+
+    def load(i):
+        span = pl.ds(i * load_rows, load_rows)
+        return pltpu.make_async_copy(patches_ref.at[0, 0, span], x_ref.at[span], load_sems.at[i])
+
+    for i in range(loads):
+        load(i).start()
+
+    def set_order():
+        start = jnp.int32(0)
+        for h in range(n_grp):
+            start += jnp.where(h < group, counts[col, h], 0)
+        to = lax.broadcasted_iota(jnp.int32, (tile, tile), 0)
+        source = (to & (each - 1)) * n_grp + (((to >> (each.bit_length() - 1)) - start) & (n_grp - 1))
+        hit = source == lax.broadcasted_iota(jnp.int32, (tile, tile), 1)
+        order[...] = hit.astype(F32).astype(BF16)
+
+    def sort_rows(low, high):
+        for c in range(low // each, high // each):
+            moved = dot(order[...], x_ref[c * tile : (c + 1) * tile, :]).astype(BF16)
+            send_ref[:, c * each : (c + 1) * each, :] = moved.reshape(n_grp, each, EMBED)
+
+    def find_picks():
+        slots = jnp.full((1, BLOCK), -1, jnp.int32)
+        for r in range(ROUNDS):
+            slots = jnp.where(owner[r] == me, slot_ref[r : r + 1, :], slots)
+        wanted = jnp.broadcast_to(slots, (BLOCK, BLOCK)).T
+        wanted -= lax.broadcasted_iota(jnp.int32, (BLOCK, BLOCK), 1)
+        unroll = 8
+
+        def look(i, acc):
+            for u in range(unroll):
+                at = pl.multiple_of((i * unroll + u) * BLOCK, BLOCK)
+                hit = (wanted == at).astype(F32).astype(BF16)
+                acc += dot(hit, x_ref[pl.ds(at, BLOCK), :])
+            return acc
+
+        found = lax.fori_loop(
+            0, x_ref.shape[0] // (unroll * BLOCK), look, jnp.zeros((BLOCK, EMBED), F32)
+        )
+        for r in range(ROUNDS):
+            mine = jnp.where(owner[r] == me, found, 0.0).astype(BF16)
+            per_round = BLOCK // PART_ROWS
+            picks_ref[r * per_round : (r + 1) * per_round] = mine.reshape(per_round, PART_ROWS, EMBED)
 
     def rows(piece, d):
         span = pl.ds(edges[piece], edges[piece + 1] - edges[piece])
@@ -249,6 +221,19 @@
             device_id_type=MESH,
         )
 
+    def before():
+        set_order()
+        for i in range(FIRST_ROWS * n_grp // load_rows):
+            load(i).wait()
+        sort_rows(0, FIRST_ROWS)
+
+    greet((("pts", n_pts), ("grp", n_grp)), place, before)
+    for d in far_first:
+        rows(0, d).start()
+    for i in range(FIRST_ROWS * n_grp // load_rows, loads):
+        load(i).wait()
+    find_picks()
+
     def scatter(d):
         target = lax.rem(col + d, n_pts)
         return target, pltpu.make_async_remote_copy(
@@ -287,10 +272,9 @@
         def _():
             copy.start()
 
+    sort_rows(FIRST_ROWS, per_peer)
     own = pltpu.make_async_copy(send_ref.at[group], got_ref.at[group], own_sem)
     own.start()
-    for d in order:
-        rows(0, d).start()
 
     @pl.when(col < PARTS)
     def _():
@@ -302,7 +286,7 @@
         for d in range(1, n_grp):
             across(d).start()
 
-    for d in order:
+    for d in far_first:
         rows(1, d).start()
 
     @pl.when(col < PARTS)
@@ -341,22 +325,33 @@
 
     own.wait()
     for piece in range(2):
-        for d in order:
+        for d in far_first:
             rows(piece, d).wait()
 
 
-def exchange(send, picks, n_grp, n_pts):
+def exchange(patches, counts, pick_slot, block_owner, n_grp, n_pts):
+    slots = patches.shape[2]
     shape = (PARTS, PART_ROWS, EMBED)
     square = (ROUNDS, ROUNDS, BLOCK, BLOCK)
+    messages = (n_grp, slots // n_grp, EMBED)
     return pl.pallas_call(
         functools.partial(exchange_kernel, n_grp, n_pts),
         out_shape=(
-            jax.ShapeDtypeStruct(send.shape, BF16),
+            jax.ShapeDtypeStruct(messages, BF16),
             jax.ShapeDtypeStruct((2 * FACTOR + EMBED, FACTOR), BF16),
         ),
-        in_specs=[pl.BlockSpec(memory_space=pltpu.HBM), pl.BlockSpec(memory_space=pltpu.VMEM)],
+        in_specs=[
+            pl.BlockSpec(memory_space=pltpu.SMEM),
+            pl.BlockSpec(memory_space=pltpu.SMEM),
+            pl.BlockSpec(memory_space=pltpu.VMEM),
+            pl.BlockSpec(memory_space=pltpu.HBM),
+        ],
         out_specs=(pl.BlockSpec(memory_space=pltpu.HBM), pl.BlockSpec(memory_space=pltpu.VMEM)),
         scratch_shapes=[
+            pltpu.VMEM((slots, EMBED), BF16),
+            pltpu.VMEM(messages, BF16),
+            pltpu.VMEM((n_grp * 16, n_grp * 16), BF16),
+            pltpu.VMEM(shape, BF16),
             pltpu.VMEM((n_pts - 1,) + shape[1:], BF16),
             pltpu.VMEM((n_grp - 1,) + shape[1:], BF16),
             pltpu.VMEM((2,) + shape[1:], BF16),
@@ -364,20 +359,21 @@
             pltpu.VMEM(square, F32),
             pltpu.VMEM((BLOCK, BLOCK), F32),
             pltpu.VMEM(square, F32),
+            pltpu.SemaphoreType.DMA((8,)),
             pltpu.SemaphoreType.DMA,
         ]
         + [pltpu.SemaphoreType.DMA((n,)) for n in (n_pts, n_pts, n_grp, n_grp, n_pts, n_pts)]
         + [pltpu.SemaphoreType.DMA((n_grp,))] * 4,
         compiler_params=pltpu.CompilerParams(
-            collective_id=0, has_side_effects=True, vmem_limit_bytes=24 << 20
+            collective_id=0, has_side_effects=True, vmem_limit_bytes=58 << 20
         ),
         name="exchange",
-    )(send, picks.reshape(shape))
+    )(counts, block_owner, pick_slot, patches)
 
 
 def factor_kernel(
     n_grp, n_pts, chunk, counts, owner, slot_ref, got_ref, weights_ref,
-    out_ref, gain_ref, points, spots, shift_ref,
+    out_ref, gain_ref, points, spots, shift_ref, doubled,
 ):
     step = pl.program_id(0)
     rows = out_ref.shape[2]
@@ -409,6 +405,9 @@
             here = (own_col == col) & ((rank & (n_grp - 1)) == group)
             spots[0:1, r * BLOCK : (r + 1) * BLOCK] = jnp.where(here, rank >> (n_grp.bit_length() - 1), -1)
 
+        corner = weights_ref[2 * BLOCK : FACTOR, 2 * BLOCK :]
+        doubled[0:BLOCK, :] = corner
+        doubled[BLOCK:, :] = corner
         twice = weights_ref[2 * FACTOR :, :].astype(F32)
         twice_high, twice_low = halves(twice * twice)
         ones = jnp.ones((8, EMBED), BF16)
@@ -422,11 +421,11 @@
     sq = jnp.concatenate(halves(wide * wide), axis=1)
     sq = dot(sq, jnp.ones((2 * EMBED, BLOCK), BF16))
     spot = lax.broadcasted_iota(jnp.int32, (rows, BLOCK), 0) + base
+    inner = dot(x, twice_ref[...])
     high, low = [], []
     for r in range(ROUNDS):
         at = slice(r * BLOCK, (r + 1) * BLOCK)
-        inner = dot(x, twice_ref[:, at])
-        part = jnp.exp2(EXP_SCALE * (inner - sq) + shift_ref[0:1, at])
+        part = jnp.exp2(EXP_SCALE * (inner[:, at] - sq) + shift_ref[0:1, at])
         part = part + jnp.where(spot == spots[0:1, at], JITTER, 0.0)
         a, b = halves(part)
         high.append(a)
@@ -440,8 +439,7 @@
         + dot(high01, low_ref[0:both, :])
     )
     last = (
-        dot(high[2], high_ref[both:, both:])
-        + dot(low[2], high_ref[both:, both:])
+        dot(jnp.concatenate([high[2], low[2]], axis=1), doubled[...])
         + dot(high[2], low_ref[both:, both:])
     )
     parts = [first[:, 0:BLOCK], first[:, BLOCK:both], first[:, both:] + last]
@@ -479,16 +477,16 @@
             pltpu.VMEM((points + chunk, EMBED), F32),
             pltpu.VMEM((1, FACTOR), jnp.int32),
             pltpu.VMEM((1, FACTOR), F32),
+            pltpu.VMEM((2 * BLOCK, BLOCK), BF16),
         ],
-        compiler_params=pltpu.CompilerParams(vmem_limit_bytes=40 << 20),
+        compiler_params=pltpu.CompilerParams(vmem_limit_bytes=58 << 20),
         name="factorize",
     )(counts, block_owner, pick_slot, got, weights)
 
 
 def per_device(patches, counts, pick_slot, block_owner):
     n_grp, n_pts = lax.axis_size("grp"), lax.axis_size("pts")
-    send, picks = pack(patches, counts, pick_slot, block_owner, n_grp, n_pts)
-    got, weights = exchange(send, picks, n_grp, n_pts)
+    got, weights = exchange(patches, counts, pick_slot, block_owner, n_grp, n_pts)
     rows, gain = factorize(got, counts, pick_slot, block_owner, weights, n_grp, n_pts)
     return rows, gain[None]
 

time: 140 us -> 129 us (0.921)
  Pallas kernels: 135 us -> 128 us
  local copies, waits for them, and re-layouts: 3.09 us -> 0 us
    pallas_call x1 -> x0, Pallas kernels: 8.19 us -> none  [pack(): pl.pallas_call(functools.partial(pack_kernel, n_grp, n_pts), grid=(steps,...]
    unnamed x10 -> x0, local copies, waits for them, and re-layouts: 3.09 us -> none
    pallas_call x1, Pallas kernels: 105 us -> 107 us  [exchange(): pl.pallas_call(functools.partial(exchange_kernel, n_grp, n_pts), out_shap...]
where the time goes in v3:
time: 129 us
  Pallas kernels  128 us (99%)
    pallas_call x1, Pallas kernels, exchange(): pl.pallas_call(functools.partial(exchange_kernel, n_grp, n_pts), out_shap...  107 us
    pallas_call x1, Pallas kernels, factorize(): pl.pallas_call(functools.partial(factor_kernel, n_grp, n_pts, chunk), gri...  21.3 us

profile of v3, /device:TPU:1, one launch (start us, length us, event | category | flops | bytes accessed | tf_op | source)
XLA Modules:
  0.0 128.6 jit_solution(2660701575156881018)
XLA Ops:
  0.6 106.7 %exchange.1 = (bf16[16,1024,128]{2,1,0:T(8,128)(2,1)}, bf16[896,384]{1,0:T(8,128)(2,1)}) custom-call(s32[16,16]{1,0:T(8,128)} %counts.3, s32[3]{0:T(128)} %owner.3, s32[3,128]{1,0:T(4,128)} %slot_ref.3, bf16[1,1,16384,128]{3,2,1,0:T(8,128)(2,1)} %patches_ref.1), custom_call_target="tpu_custom_call" | custom-call | tf_op jit(solution)/shard_map/exchange/pallas_call | solution.py:337
  107.3 21.3 %factorize.1 = (bf16[1,1,8192,384]{3,2,1,0:T(8,128)(2,1)}, f32[1,8192]{1,0:T(1,128)}) custom-call(s32[16,16]{1,0:T(8,128)} %counts.3, s32[3]{0:T(128)} %owner.3, s32[3,128]{1,0:T(4,128)} %slot_ref.3, bf16[16,1024,128]{2,1,0:T(8,128)(2,1)} %get-tuple-element.6.got_ref, bf16[896,384]{1,0:T(8,128)(2,1)} %get-tuple-element.7.weights_ref), custom_call_target="tpu_custom_call" | custom-call | tf_op jit(solution)/shard_map/factorize/pallas_call | solution.py:458

commit v4 on v3

v4 whole, which is shorter than its diff:
```python
import functools
import math

import jax
import jax.numpy as jnp
from jax import lax
from jax.experimental import pallas as pl
from jax.experimental.pallas import tpu as pltpu
from jax.sharding import PartitionSpec as P

MESH = pl.DeviceIdType.MESH
HIGHEST = lax.Precision.HIGHEST
JITTER = 0.1
EMBED = 128
BLOCK = 128
ROUNDS = 3
FACTOR = ROUNDS * BLOCK
PARTS = 12
PART_ROWS = FACTOR // PARTS
FIRST_ROWS = 256
EARLY_ROWS = 704
SOURCES = 3
EXP_SCALE = math.log2(math.e) / EMBED
F32 = jnp.float32
BF16 = jnp.bfloat16


def dot(a, b, precision=None):
    return jnp.dot(a, b, precision=precision, preferred_element_type=F32)


def dot_nt(a, b, precision=None):
    return lax.dot_general(
        a, b, (((1,), (1,)), ((), ())), precision=precision, preferred_element_type=F32
    )


def halves(x):
    high = x.astype(BF16)
    return high, (x - high.astype(F32)).astype(BF16)


def greet(axis_sizes, place, meanwhile):
    barrier = pltpu.get_barrier_semaphore()
    total = 0
    for axis, size in axis_sizes:
        for d in range(1, size):
            pl.semaphore_signal(barrier, inc=1, device_id=place(axis, d), device_id_type=MESH)
        total += size - 1
    meanwhile()
    pl.semaphore_wait(barrier, total)


def neighbour(n_grp, n_pts):
    group, col = lax.axis_index("grp"), lax.axis_index("pts")

    def place(axis, d):
        if axis == "grp":
            return (lax.rem(group + d, n_grp), col)
        return (group, lax.rem(col + d, n_pts))

    return place


def unit_inverse(a_ref, m_ref):
    sub = lax.broadcasted_iota(jnp.int32, (8, BLOCK), 0)
    m_ref[...] = (
        lax.broadcasted_iota(jnp.int32, (BLOCK, BLOCK), 0)
        == lax.broadcasted_iota(jnp.int32, (BLOCK, BLOCK), 1)
    ).astype(F32)

    def row(x, k):
        return jnp.broadcast_to(x[k : k + 1, :], (8, BLOCK))

    for b in range(BLOCK // 8):
        low = 8 * b
        pa = a_ref[low : low + 8, :]
        pm = m_ref[low : low + 8, :]
        cols = [jnp.broadcast_to(pa[:, low + j : low + j + 1], (8, BLOCK)) for j in range(8)]
        pivots = jnp.ones((8, BLOCK), F32)
        inverses = pivots
        for k in range(8):
            pivot = row(cols[k], k)
            inverse = 1.0 / pivot
            pivots = jnp.where(sub == k, pivot, pivots)
            inverses = jnp.where(sub == k, inverse, inverses)
            if k < 7:
                f = jnp.where(sub > k, cols[k] * inverse, 0.0)
                for j in range(k + 1, 8):
                    cols[j] = cols[j] - f * row(cols[j], k)
                pa = pa - f * row(pa, k)
                pm = pm - f * row(pm, k)
        if b < BLOCK // 8 - 1:
            below = pa.T[low + 8 :, :]
            a_ref[low + 8 :, :] -= dot(below, pa * inverses, HIGHEST)
            m_ref[low + 8 :, :] -= dot(below, pm * inverses, HIGHEST)
        scale = lax.rsqrt(pivots)
        scale = scale * (1.5 - 0.5 * pivots * scale * scale)
        m_ref[low : low + 8, :] = pm * scale


def prepare(blocks, weights_ref, schur, work, inv):
    wide = blocks.astype(F32)
    sq_high, sq_low = halves(wide * wide)
    ones = jnp.ones((EMBED, BLOCK), BF16)
    sq_col = dot(sq_high, ones) + dot(sq_low, ones)
    row_ones = jnp.ones((8, EMBED), BF16)
    sq_row = (dot_nt(row_ones, sq_high) + dot_nt(row_ones, sq_low))[0:1, :]
    weights_ref[2 * FACTOR :, :] = (2.0 * wide).T.astype(BF16)
    eye = (
        lax.broadcasted_iota(jnp.int32, (BLOCK, BLOCK), 0)
        == lax.broadcasted_iota(jnp.int32, (BLOCK, BLOCK), 1)
    )
    def span(i):
        return slice(i * BLOCK, (i + 1) * BLOCK)

    for i in range(ROUNDS):
        for j in range(i + 1):
            inner = dot_nt(blocks[span(i)], blocks[span(j)])
            dist = 2.0 * inner - sq_col[span(i)] - sq_row[:, span(j)]
            part = jnp.exp2(EXP_SCALE * dist)
            if i == j:
                part = part + jnp.where(eye, JITTER, 0.0)
            schur[i, j] = part

    for r in range(ROUNDS):
        work[...] = schur[r, r]
        unit_inverse(work, inv.at[r, r])
        for i in range(r + 1, ROUNDS):
            schur[i, r] = dot_nt(schur[i, r], inv[r, r], HIGHEST)
        for i in range(r + 1, ROUNDS):
            for j in range(r + 1, i + 1):
                schur[i, j] -= dot_nt(schur[i, r], schur[j, r], HIGHEST)

    inv[1, 0] = -dot(inv[1, 1], dot(schur[1, 0], inv[0, 0], HIGHEST), HIGHEST)
    inv[2, 1] = -dot(inv[2, 2], dot(schur[2, 1], inv[1, 1], HIGHEST), HIGHEST)
    inv[2, 0] = -dot(
        inv[2, 2],
        dot(schur[2, 0], inv[0, 0], HIGHEST) + dot(schur[2, 1], inv[1, 0], HIGHEST),
        HIGHEST,
    )
    for i in range(ROUNDS):
        for j in range(ROUNDS):
            if j <= i:
                high, low = halves(inv[i, j].T)
            else:
                high = low = jnp.zeros((BLOCK, BLOCK), BF16)
            weights_ref[span(j), span(i)] = high
            weights_ref[span(ROUNDS + j), span(i)] = low


def segment(counts, col, group, h, start, n_grp):
    odd = start & (n_grp - 1)
    begin = lax.div(start, n_grp) + jnp.where(group < odd, 1, 0)
    first = (group - odd) & (n_grp - 1)
    number = jnp.maximum(lax.div(counts[col, h] - first + n_grp - 1, n_grp), 0)
    return begin, number


def set_up(n_grp, n_pts, counts, owner, slot_ref, weights_ref, spots, shift_ref, doubled):
    group, col = lax.axis_index("grp"), lax.axis_index("pts")
    for r in range(ROUNDS):
        own_group, own_col = lax.div(owner[r], n_pts), lax.rem(owner[r], n_pts)
        begin = jnp.int32(0)
        for h in range(n_grp):
            begin += jnp.where(h < own_group, counts[own_col, h], 0)
        rank = begin + slot_ref[r : r + 1, :]
        here = (own_col == col) & ((rank & (n_grp - 1)) == group)
        spots[0:1, r * BLOCK : (r + 1) * BLOCK] = jnp.where(
            here, rank >> (n_grp.bit_length() - 1), -1
        )
    corner = weights_ref[2 * BLOCK : FACTOR, 2 * BLOCK :]
    doubled[0:BLOCK, :] = corner
    doubled[BLOCK:, :] = corner
    twice = weights_ref[2 * FACTOR :, :].astype(F32)
    high, low = halves(twice * twice)
    ones = jnp.ones((8, EMBED), BF16)
    shift_ref[...] = (-0.25 * EXP_SCALE) * (dot(ones, high) + dot(ones, low))[0:1, :]


def factor_rows(wide, base, weights_ref, spots, shift_ref, doubled):
    rows = wide.shape[0]
    high_ref, low_ref = weights_ref.at[0:FACTOR], weights_ref.at[FACTOR : 2 * FACTOR]
    twice_ref = weights_ref.at[2 * FACTOR :]
    x = wide.astype(BF16)
    sq = jnp.concatenate(halves(wide * wide), axis=1)
    sq = dot(sq, jnp.ones((2 * EMBED, BLOCK), BF16))
    spot = lax.broadcasted_iota(jnp.int32, (rows, BLOCK), 0) + base
    inner = dot(x, twice_ref[...])
    high, low = [], []
    for r in range(ROUNDS):
        at = slice(r * BLOCK, (r + 1) * BLOCK)
        part = jnp.exp2(EXP_SCALE * (inner[:, at] - sq) + shift_ref[0:1, at])
        part = part + jnp.where(spot == spots[0:1, at], JITTER, 0.0)
        a, b = halves(part)
        high.append(a)
        low.append(b)
    both = 2 * BLOCK
    high01 = jnp.concatenate(high[:2], axis=1)
    low01 = jnp.concatenate(low[:2], axis=1)
    first = (
        dot(high01, high_ref[0:both, :])
        + dot(low01, high_ref[0:both, :])
        + dot(high01, low_ref[0:both, :])
    )
    last = (
        dot(jnp.concatenate([high[2], low[2]], axis=1), doubled[...])
        + dot(high[2], low_ref[both:, both:])
    )
    parts = [first[:, 0:BLOCK], first[:, BLOCK:both], first[:, both:] + last]
    square = parts[0] * parts[0] + parts[1] * parts[1] + parts[2] * parts[2]
    square = jnp.concatenate(halves(square), axis=1)
    gain = (1.0 + JITTER) - dot_nt(jnp.ones((8, 2 * BLOCK), BF16), square)[0:1, :]
    return [p.astype(BF16) for p in parts], gain


def tabulate(counts, begins, numbers, n_grp):
    group, col = lax.axis_index("grp"), lax.axis_index("pts")
    start = jnp.int32(0)
    for h in range(n_grp):
        begin, number = segment(counts, col, group, h, start, n_grp)
        begins[h] = begin
        numbers[h] = number
        start += counts[col, h]


def first_source(begins, numbers, base, n_grp):
    source = jnp.int32(0)
    for h in range(n_grp):
        source += jnp.where(begins[h] + numbers[h] <= base, 1, 0)
    return jnp.minimum(source, n_grp - 1)


def exchange_kernel(
    n_grp, n_pts, counts, owner, slot_ref, patches_ref, got_ref, weights_ref, early_ref, gain_ref,
    spread_out, local, staged, points, begins, numbers, spots, shift_ref, doubled, local_sem, out_sems,
    x_ref, send_ref, order, picks_ref, got1, got2, part, gathered, schur, work, inv,
    load_sems, own_sem, *sems,
):
    group, col = lax.axis_index("grp"), lax.axis_index("pts")
    me = group * n_pts + col
    place = neighbour(n_grp, n_pts)
    (s1, r1), (s2, r2), (s3, r3) = sems[0:2], sems[2:4], sems[4:6]
    bulk = sems[6:]
    per_peer = send_ref.shape[1]
    edges = (0, FIRST_ROWS, EARLY_ROWS, per_peer)
    tile = order.shape[0]
    each = tile // n_grp
    loads = load_sems.shape[0]
    load_rows = x_ref.shape[0] // loads
    far_first = sorted(range(1, n_grp), key=lambda d: -min(d, n_grp - d))

    def load(i):
        span = pl.ds(i * load_rows, load_rows)
        return pltpu.make_async_copy(patches_ref.at[0, 0, span], x_ref.at[span], load_sems.at[i])

    for i in range(loads):
        load(i).start()

    def set_order():
        start = jnp.int32(0)
        for h in range(n_grp):
            start += jnp.where(h < group, counts[col, h], 0)
        to = lax.broadcasted_iota(jnp.int32, (tile, tile), 0)
        source = (to & (each - 1)) * n_grp + (((to >> (each.bit_length() - 1)) - start) & (n_grp - 1))
        hit = source == lax.broadcasted_iota(jnp.int32, (tile, tile), 1)
        order[...] = hit.astype(F32).astype(BF16)

    def sort_rows(low, high):
        for c in range(low // each, high // each):
            moved = dot(order[...], x_ref[c * tile : (c + 1) * tile, :]).astype(BF16)
            send_ref[:, c * each : (c + 1) * each, :] = moved.reshape(n_grp, each, EMBED)

    def find_picks():
        slots = jnp.full((1, BLOCK), -1, jnp.int32)
        for r in range(ROUNDS):
            slots = jnp.where(owner[r] == me, slot_ref[r : r + 1, :], slots)
        wanted = jnp.broadcast_to(slots, (BLOCK, BLOCK)).T
        wanted -= lax.broadcasted_iota(jnp.int32, (BLOCK, BLOCK), 1)
        unroll = 8

        def look(i, acc):
            for u in range(unroll):
                at = pl.multiple_of((i * unroll + u) * BLOCK, BLOCK)
                hit = (wanted == at).astype(F32).astype(BF16)
                acc += dot(hit, x_ref[pl.ds(at, BLOCK), :])
            return acc

        found = lax.fori_loop(
            0, x_ref.shape[0] // (unroll * BLOCK), look, jnp.zeros((BLOCK, EMBED), F32)
        )
        for r in range(ROUNDS):
            mine = jnp.where(owner[r] == me, found, 0.0).astype(BF16)
            per_round = BLOCK // PART_ROWS
            picks_ref[r * per_round : (r + 1) * per_round] = mine.reshape(per_round, PART_ROWS, EMBED)

    def rows(piece, d):
        span = pl.ds(edges[piece], edges[piece + 1] - edges[piece])
        target = lax.rem(group + d, n_grp)
        return pltpu.make_async_remote_copy(
            src_ref=send_ref.at[target, span],
            dst_ref=got_ref.at[group, span],
            send_sem=bulk[2 * piece].at[d],
            recv_sem=bulk[2 * piece + 1].at[d],
            device_id=place("grp", d),
            device_id_type=MESH,
        )

    def before():
        set_order()
        for i in range(FIRST_ROWS * n_grp // load_rows):
            load(i).wait()
        sort_rows(0, FIRST_ROWS)

    greet((("pts", n_pts), ("grp", n_grp)), place, before)
    for d in far_first:
        rows(0, d).start()
    for i in range(FIRST_ROWS * n_grp // load_rows, loads):
        load(i).wait()
    find_picks()

    def scatter(d):
        target = lax.rem(col + d, n_pts)
        return target, pltpu.make_async_remote_copy(
            src_ref=picks_ref.at[jnp.minimum(target, PARTS - 1)],
            dst_ref=got1.at[d - 1],
            send_sem=s1.at[d],
            recv_sem=r1.at[d],
            device_id=place("pts", d),
            device_id_type=MESH,
        )

    def across(d):
        return pltpu.make_async_remote_copy(
            src_ref=part.at[0],
            dst_ref=got2.at[d - 1],
            send_sem=s2.at[d],
            recv_sem=r2.at[d],
            device_id=place("grp", d),
            device_id_type=MESH,
        )

    def gather(d, owner):
        return pltpu.make_async_remote_copy(
            src_ref=part.at[1],
            dst_ref=gathered.at[owner],
            send_sem=s3.at[d],
            recv_sem=r3.at[d],
            device_id=place("pts", d),
            device_id_type=MESH,
        )

    for d in range(1, n_pts):
        target, copy = scatter(d)

        @pl.when(target < PARTS)
        def _():
            copy.start()

    sort_rows(FIRST_ROWS, per_peer)
    own = pltpu.make_async_copy(send_ref.at[group], got_ref.at[group], own_sem)
    own.start()

    @pl.when(col < PARTS)
    def _():
        acc = picks_ref[jnp.minimum(col, PARTS - 1)].astype(F32)
        for d in range(1, n_pts):
            scatter(d)[1].wait_recv()
            acc += got1[d - 1].astype(F32)
        part[0] = acc.astype(BF16)
        for d in range(1, n_grp):
            across(d).start()

    for piece in (1, 2):
        for d in far_first:
            rows(piece, d).start()

    @pl.when(col < PARTS)
    def _():
        acc = part[0].astype(F32)
        for d in range(1, n_grp):
            across(d).wait_recv()
            acc += got2[d - 1].astype(F32)
        part[1] = acc.astype(BF16)
        for d in range(1, n_pts):
            gather(d, col).start()
        gathered[col] = part[1]

    for d in range(1, n_pts):
        source = lax.rem(col + n_pts - d, n_pts)

        @pl.when(source < PARTS)
        def _():
            gather(d, source).wait_recv()

    prepare(gathered[...].reshape(FACTOR, EMBED), weights_ref, schur, work, inv)
    set_up(n_grp, n_pts, counts, owner, slot_ref, weights_ref, spots, shift_ref, doubled)
    tabulate(counts, begins, numbers, n_grp)
    spread_out[:, 0:BLOCK, :] = jnp.zeros((n_grp, BLOCK, EMBED), F32)
    spread_out[:, BLOCK + EARLY_ROWS :, :] = jnp.zeros((n_grp, BLOCK, EMBED), F32)

    own.wait()
    for piece in (0, 1):
        for d in far_first:
            rows(piece, d).wait_recv()
    fetch = pltpu.make_async_copy(got_ref.at[:, pl.ds(0, EARLY_ROWS)], local, local_sem)
    fetch.start()
    fetch.wait()

    def widen(h, _):
        spread_out[h, BLOCK : BLOCK + EARLY_ROWS, :] = local[h].astype(F32)
        return 0

    lax.fori_loop(0, n_grp, widen, 0)
    row = lax.broadcasted_iota(jnp.int32, (BLOCK, EMBED), 0)
    step_rows = points.shape[0]

    per_step = step_rows // BLOCK

    def out_copy(i):
        span = pl.ds(i * per_step, per_step)
        return pltpu.make_async_copy(staged.at[span], early_ref.at[span], out_sems.at[i])

    def early(i, _):
        base = pl.multiple_of(i * step_rows, step_rows)
        for b in range(step_rows // BLOCK):
            first = first_source(begins, numbers, base + b * BLOCK, n_grp)
            x = jnp.zeros((BLOCK, EMBED), F32)
            for k in range(SOURCES):
                source = jnp.minimum(first + k, n_grp - 1)
                skip = base + b * BLOCK - begins[source]
                limit = jnp.minimum(numbers[source], EARLY_ROWS)
                at = jnp.clip(skip, -BLOCK, EARLY_ROWS) + BLOCK
                new = spread_out[source, pl.ds(at, BLOCK), :]
                x = jnp.where((row + skip >= 0) & (row + skip < limit), new, x)
            points[b * BLOCK : (b + 1) * BLOCK, :] = x
        parts, gain = factor_rows(points[...], base, weights_ref, spots, shift_ref, doubled)
        for b in range(per_step):
            for r in range(ROUNDS):
                staged[i * per_step + b, :, r * BLOCK : (r + 1) * BLOCK] = parts[r][
                    b * BLOCK : (b + 1) * BLOCK, :
                ]
            gain_ref[pl.ds(i * (step_rows // BLOCK) + b, 1), :] = gain[:, b * BLOCK : (b + 1) * BLOCK]
        out_copy(i).start()
        return 0

    lax.fori_loop(0, out_sems.shape[0], early, 0)

    for d in range(1, n_pts):
        target, copy = scatter(d)

        @pl.when(target < PARTS)
        def _():
            copy.wait_send()

    @pl.when(col < PARTS)
    def _():
        for d in range(1, n_grp):
            across(d).wait_send()
        for d in range(1, n_pts):
            gather(d, col).wait_send()

    def finish(i, _):
        out_copy(i).wait()
        return 0

    lax.fori_loop(0, out_sems.shape[0], finish, 0)
    for d in far_first:
        rows(2, d).wait_recv()
    for piece in range(3):
        for d in far_first:
            rows(piece, d).wait_send()


def exchange(patches, counts, pick_slot, block_owner, n_grp, n_pts):
    slots = patches.shape[2]
    shape = (PARTS, PART_ROWS, EMBED)
    square = (ROUNDS, ROUNDS, BLOCK, BLOCK)
    messages = (n_grp, slots // n_grp, EMBED)
    points = slots // 2
    rows = 512
    return pl.pallas_call(
        functools.partial(exchange_kernel, n_grp, n_pts),
        out_shape=(
            jax.ShapeDtypeStruct(messages, BF16),
            jax.ShapeDtypeStruct((2 * FACTOR + EMBED, FACTOR), BF16),
            jax.ShapeDtypeStruct((points // BLOCK, BLOCK, FACTOR), BF16),
            jax.ShapeDtypeStruct((points // BLOCK, BLOCK), F32),
        ),
        in_specs=[
            pl.BlockSpec(memory_space=pltpu.SMEM),
            pl.BlockSpec(memory_space=pltpu.SMEM),
            pl.BlockSpec(memory_space=pltpu.VMEM),
            pl.BlockSpec(memory_space=pltpu.HBM),
        ],
        out_specs=(
            pl.BlockSpec(memory_space=pltpu.HBM),
            pl.BlockSpec(memory_space=pltpu.VMEM),
            pl.BlockSpec(memory_space=pltpu.HBM),
            pl.BlockSpec(memory_space=pltpu.VMEM),
        ),
        scratch_shapes=[
            pltpu.VMEM((n_grp, EARLY_ROWS + 2 * BLOCK, EMBED), F32),
            pltpu.VMEM((n_grp, EARLY_ROWS, EMBED), BF16),
            pltpu.VMEM((points // BLOCK, BLOCK, FACTOR), BF16),
            pltpu.VMEM((rows, EMBED), F32),
            pltpu.SMEM((n_grp,), jnp.int32),
            pltpu.SMEM((n_grp,), jnp.int32),
            pltpu.VMEM((1, FACTOR), jnp.int32),
            pltpu.VMEM((1, FACTOR), F32),
            pltpu.VMEM((2 * BLOCK, BLOCK), BF16),
            pltpu.SemaphoreType.DMA,
            pltpu.SemaphoreType.DMA((points // rows,)),
            pltpu.VMEM((slots, EMBED), BF16),
            pltpu.VMEM(messages, BF16),
            pltpu.VMEM((n_grp * 16, n_grp * 16), BF16),
            pltpu.VMEM(shape, BF16),
            pltpu.VMEM((n_pts - 1,) + shape[1:], BF16),
            pltpu.VMEM((n_grp - 1,) + shape[1:], BF16),
            pltpu.VMEM((2,) + shape[1:], BF16),
            pltpu.VMEM(shape, BF16),
            pltpu.VMEM(square, F32),
            pltpu.VMEM((BLOCK, BLOCK), F32),
            pltpu.VMEM(square, F32),
            pltpu.SemaphoreType.DMA((8,)),
            pltpu.SemaphoreType.DMA,
        ]
        + [pltpu.SemaphoreType.DMA((n,)) for n in (n_pts, n_pts, n_grp, n_grp, n_pts, n_pts)]
        + [pltpu.SemaphoreType.DMA((n_grp,))] * 6,
        compiler_params=pltpu.CompilerParams(
            collective_id=0, has_side_effects=True, vmem_limit_bytes=58 << 20
        ),
        name="exchange",
    )(counts, block_owner, pick_slot, patches)


def late_kernel(
    n_grp, n_pts, counts, owner, slot_ref, got_in, weights_ref, gain_in, early_ref,
    out_ref, gain_ref, got_ref, window, staged, begins, numbers, flags, spots, shift_ref, doubled, in_sems, sems,
):
    in_early = pltpu.make_async_copy(early_ref, staged, in_sems.at[0])
    in_early.start()
    in_got = pltpu.make_async_copy(got_in, got_ref, in_sems.at[1])
    in_got.start()
    per_peer = got_ref.shape[1]
    n_blocks = gain_ref.shape[0]
    reach = BLOCK + 16
    gain_ref[...] = gain_in[...]
    tabulate(counts, begins, numbers, n_grp)
    for b in range(n_blocks):
        flags[b] = 0
    for h in range(n_grp):
        end = begins[h] + numbers[h]

        def mark(b, _):
            flags[b] = 1
            return 0

        low = lax.div(begins[h] + EARLY_ROWS, BLOCK)
        high = jnp.where(numbers[h] > EARLY_ROWS, lax.div(end - 1, BLOCK) + 1, low)
        lax.fori_loop(low, high, mark, 0)
        if h + SOURCES < n_grp:
            last = lax.div(jnp.maximum(end - 1, 0), BLOCK)

            @pl.when(last == lax.div(begins[h + SOURCES], BLOCK))
            def _():
                flags[last] = 1

    def span(b):
        return pl.ds(pl.multiple_of(b * BLOCK, BLOCK), BLOCK)

    def copy_new(b):
        return pltpu.make_async_copy(staged.at[b], out_ref.at[0, 0, span(b), :], sems.at[b])

    def keep(b, _):
        @pl.when(flags[b] == 0)
        def _():
            copy_new(b).start()

        return 0

    set_up(n_grp, n_pts, counts, owner, slot_ref, weights_ref, spots, shift_ref, doubled)
    window[...] = jnp.zeros_like(window)
    in_early.wait()
    lax.fori_loop(0, n_blocks, keep, 0)
    in_got.wait()
    row = lax.broadcasted_iota(jnp.int32, (BLOCK, EMBED), 0)

    def redo(b, _):
        @pl.when(flags[b] == 1)
        def _():
            base = pl.multiple_of(b * BLOCK, BLOCK)
            first = first_source(begins, numbers, base, n_grp)
            stop = jnp.int32(0)
            for h in range(n_grp):
                stop += jnp.where(begins[h] < base + BLOCK, 1, 0)

            def add(source, x):
                skip = base - begins[source]
                at = jnp.clip((skip >> 4) << 4, 0, per_peer - reach)
                at = pl.multiple_of(at, 16)
                window[BLOCK : BLOCK + reach, :] = got_ref[source, pl.ds(at, reach), :].astype(F32)
                begin = jnp.clip(skip - at, -BLOCK, reach) + BLOCK
                new = window[pl.ds(begin, BLOCK), :]
                return jnp.where((row + skip >= 0) & (row + skip < numbers[source]), new, x)

            x = lax.fori_loop(first, stop, add, jnp.zeros((BLOCK, EMBED), F32))
            parts, gain = factor_rows(x, base, weights_ref, spots, shift_ref, doubled)
            for r in range(ROUNDS):
                staged[b, :, r * BLOCK : (r + 1) * BLOCK] = parts[r]
            gain_ref[pl.ds(b, 1), :] = gain
            copy_new(b).start()

        return 0

    lax.fori_loop(0, n_blocks, redo, 0)

    def finish(b, _):
        copy_new(b).wait()
        return 0

    lax.fori_loop(0, n_blocks, finish, 0)


def late(got, counts, pick_slot, block_owner, weights, gain, early_rows, n_grp, n_pts):
    n_blocks = gain.shape[0]
    smem = pl.BlockSpec(memory_space=pltpu.SMEM)
    vmem = pl.BlockSpec(memory_space=pltpu.VMEM)
    hbm = pl.BlockSpec(memory_space=pltpu.HBM)
    return pl.pallas_call(
        functools.partial(late_kernel, n_grp, n_pts),
        out_shape=(
            jax.ShapeDtypeStruct((1, 1, n_blocks * BLOCK, FACTOR), BF16),
            jax.ShapeDtypeStruct(gain.shape, F32),
        ),
        in_specs=[smem, smem, vmem, hbm, vmem, vmem, hbm],
        out_specs=(hbm, vmem),
        scratch_shapes=[
            pltpu.VMEM(got.shape, BF16),
            pltpu.VMEM((3 * BLOCK + 16, EMBED), F32),
            pltpu.VMEM((n_blocks, BLOCK, FACTOR), BF16),
            pltpu.SMEM((n_grp,), jnp.int32),
            pltpu.SMEM((n_grp,), jnp.int32),
            pltpu.SMEM((n_blocks,), jnp.int32),
            pltpu.VMEM((1, FACTOR), jnp.int32),
            pltpu.VMEM((1, FACTOR), F32),
            pltpu.VMEM((2 * BLOCK, BLOCK), BF16),
            pltpu.SemaphoreType.DMA((2,)),
            pltpu.SemaphoreType.DMA((n_blocks,)),
        ],
        compiler_params=pltpu.CompilerParams(vmem_limit_bytes=58 << 20),
        name="late",
    )(counts, block_owner, pick_slot, got, weights, gain, early_rows)


def per_device(patches, counts, pick_slot, block_owner):
    n_grp, n_pts = lax.axis_size("grp"), lax.axis_size("pts")
    got, weights, rows, gain = exchange(patches, counts, pick_slot, block_owner, n_grp, n_pts)
    rows, gain = late(got, counts, pick_slot, block_owner, weights, gain, rows, n_grp, n_pts)
    return rows, gain.reshape(1, 1, gain.size)


def solution(mesh):
    in_specs = (P("grp", "pts", None, None), P(), P(), P())
    out_specs = (P("grp", "pts", None, None), P("grp", "pts", None))
    return jax.shard_map(
        per_device, mesh=mesh, in_specs=in_specs, out_specs=out_specs, check_vma=False
    )
```

time: 129 us -> 121 us (0.938); the launches traced: 129 us -> 119 us
  Pallas kernels: 128 us -> 118 us
    pallas_call x1, Pallas kernels: 21.3 us -> 9.69 us  [late(): pl.pallas_call(functools.partial(late_kernel, n_grp, n_pts), out_shape=(j...]
    pallas_call x1, Pallas kernels: 107 us -> 109 us  [exchange(): pl.pallas_call(functools.partial(exchange_kernel, n_grp, n_pts), out_shap...]
where the time goes in v4:
time: 121 us; the launch traced here: 119 us
  Pallas kernels  118 us (98%)
    pallas_call x1, Pallas kernels, exchange(): pl.pallas_call(functools.partial(exchange_kernel, n_grp, n_pts), out_shap...  109 us
    pallas_call x1, Pallas kernels, late(): pl.pallas_call(functools.partial(late_kernel, n_grp, n_pts), out_shape=(j...  9.69 us

profile of v4, /device:TPU:1, one launch (start us, length us, event | category | flops | bytes accessed | tf_op | source)
XLA Modules:
  0.0 119.1 jit_solution(1892929520484399977)
XLA Ops:
  0.6 108.6 %exchange.1 = (bf16[16,1024,128]{2,1,0:T(8,128)(2,1)}, bf16[896,384]{1,0:T(8,128)(2,1)}, bf16[64,128,384]{2,1,0:T(8,128)(2,1)}, f32[64,128]{1,0:T(8,128)}) custom-call(s32[16,16]{1,0:T(8,128)} %counts.3, s32[3]{0:T(128)} %owner.3, s32[3,128]{1,0:T(4,128)} %slot_ref.3, bf16[1,1,16384,128]{3,2,1,0:T(8,128)(2,1)} %patches_ref.1), custom_call_target="tpu_custom_call" | custom-call | tf_op jit(solution)/shard_map/exchange/pallas_call | solution.py:482
  109.2 9.7 %late.1 = (bf16[1,1,8192,384]{3,2,1,0:T(8,128)(2,1)}, f32[64,128]{1,0:T(8,128)}) custom-call(s32[16,16]{1,0:T(8,128)} %counts.3, s32[3]{0:T(128)} %owner.3, s32[3,128]{1,0:T(4,128)} %slot_ref.3, bf16[16,1024,128]{2,1,0:T(8,128)(2,1)} %get-tuple-element.8.got_in, bf16[896,384]{1,0:T(8,128)(2,1)} %get-tuple-element.9.weights_ref, ...), custom_call_target="tpu_custom_call" | custom-call | tf_op jit(solution)/shard_map/late/pallas_call | solution.py:630

commit v5 on v4

--- a/solution.py
+++ b/solution.py
@@ -18,7 +18,7 @@
 PARTS = 12
 PART_ROWS = FACTOR // PARTS
 FIRST_ROWS = 256
-EARLY_ROWS = 704
+EARLY_ROWS = 768
 SOURCES = 3
 EXP_SCALE = math.log2(math.e) / EMBED
 F32 = jnp.float32
@@ -248,7 +248,7 @@
     each = tile // n_grp
     loads = load_sems.shape[0]
     load_rows = x_ref.shape[0] // loads
-    far_first = sorted(range(1, n_grp), key=lambda d: -min(d, n_grp - d))
+    near_first = sorted(range(1, n_grp), key=lambda d: min(d, n_grp - d))
 
     def load(i):
         span = pl.ds(i * load_rows, load_rows)
@@ -313,7 +313,7 @@
         sort_rows(0, FIRST_ROWS)
 
     greet((("pts", n_pts), ("grp", n_grp)), place, before)
-    for d in far_first:
+    for d in near_first:
         rows(0, d).start()
     for i in range(FIRST_ROWS * n_grp // load_rows, loads):
         load(i).wait()
@@ -372,7 +372,7 @@
             across(d).start()
 
     for piece in (1, 2):
-        for d in far_first:
+        for d in near_first:
             rows(piece, d).start()
 
     @pl.when(col < PARTS)
@@ -401,7 +401,7 @@
 
     own.wait()
     for piece in (0, 1):
-        for d in far_first:
+        for d in near_first:
             rows(piece, d).wait_recv()
     fetch = pltpu.make_async_copy(got_ref.at[:, pl.ds(0, EARLY_ROWS)], local, local_sem)
     fetch.start()
@@ -465,10 +465,10 @@
         return 0
 
     lax.fori_loop(0, out_sems.shape[0], finish, 0)
-    for d in far_first:
+    for d in near_first:
         rows(2, d).wait_recv()
     for piece in range(3):
-        for d in far_first:
+        for d in near_first:
             rows(piece, d).wait_send()
 
 

time: 121 us -> 120 us (level); the launches traced: 119 us -> 119 us
  no operation moved by 1% of the time
where the time goes in v5:
time: 120 us; the launch traced here: 119 us
  Pallas kernels  119 us (99%)
    pallas_call x1, Pallas kernels, exchange(): pl.pallas_call(functools.partial(exchange_kernel, n_grp, n_pts), out_shap...  109 us
    pallas_call x1, Pallas kernels, late(): pl.pallas_call(functools.partial(late_kernel, n_grp, n_pts), out_shape=(j...  9.27 us

profile of v5, /device:TPU:1, one launch (start us, length us, event | category | flops | bytes accessed | tf_op | source)
XLA Modules:
  0.0 119.5 jit_solution(10287472372168973739)
XLA Ops:
  0.6 109.4 %exchange.1 = (bf16[16,1024,128]{2,1,0:T(8,128)(2,1)}, bf16[896,384]{1,0:T(8,128)(2,1)}, bf16[64,128,384]{2,1,0:T(8,128)(2,1)}, f32[64,128]{1,0:T(8,128)}) custom-call(s32[16,16]{1,0:T(8,128)} %counts.3, s32[3]{0:T(128)} %owner.3, s32[3,128]{1,0:T(4,128)} %slot_ref.3, bf16[1,1,16384,128]{3,2,1,0:T(8,128)(2,1)} %patches_ref.1), custom_call_target="tpu_custom_call" | custom-call | tf_op jit(solution)/shard_map/exchange/pallas_call | solution.py:482
  110.0 9.3 %late.1 = (bf16[1,1,8192,384]{3,2,1,0:T(8,128)(2,1)}, f32[64,128]{1,0:T(8,128)}) custom-call(s32[16,16]{1,0:T(8,128)} %counts.3, s32[3]{0:T(128)} %owner.3, s32[3,128]{1,0:T(4,128)} %slot_ref.3, bf16[16,1024,128]{2,1,0:T(8,128)(2,1)} %get-tuple-element.8.got_in, bf16[896,384]{1,0:T(8,128)(2,1)} %get-tuple-element.9.weights_ref, ...), custom_call_target="tpu_custom_call" | custom-call | tf_op jit(solution)/shard_map/late/pallas_call | solution.py:630

commit v6 on v5

--- a/solution.py
+++ b/solution.py
@@ -538,9 +538,16 @@
     n_grp, n_pts, counts, owner, slot_ref, got_in, weights_ref, gain_in, early_ref,
     out_ref, gain_ref, got_ref, window, staged, begins, numbers, flags, spots, shift_ref, doubled, in_sems, sems,
 ):
-    in_early = pltpu.make_async_copy(early_ref, staged, in_sems.at[0])
-    in_early.start()
-    in_got = pltpu.make_async_copy(got_in, got_ref, in_sems.at[1])
+    shares = in_sems.shape[0] - 1
+    share = staged.shape[0] // shares
+
+    def in_early(i):
+        span = pl.ds(i * share, share)
+        return pltpu.make_async_copy(early_ref.at[span], staged.at[span], in_sems.at[i])
+
+    for i in range(shares):
+        in_early(i).start()
+    in_got = pltpu.make_async_copy(got_in, got_ref, in_sems.at[shares])
     in_got.start()
     per_peer = got_ref.shape[1]
     n_blocks = gain_ref.shape[0]
@@ -581,8 +588,9 @@
 
     set_up(n_grp, n_pts, counts, owner, slot_ref, weights_ref, spots, shift_ref, doubled)
     window[...] = jnp.zeros_like(window)
-    in_early.wait()
-    lax.fori_loop(0, n_blocks, keep, 0)
+    for i in range(shares):
+        in_early(i).wait()
+        lax.fori_loop(i * share, (i + 1) * share, keep, 0)
     in_got.wait()
     row = lax.broadcasted_iota(jnp.int32, (BLOCK, EMBED), 0)
 
@@ -645,7 +653,7 @@
             pltpu.VMEM((1, FACTOR), jnp.int32),
             pltpu.VMEM((1, FACTOR), F32),
             pltpu.VMEM((2 * BLOCK, BLOCK), BF16),
-            pltpu.SemaphoreType.DMA((2,)),
+            pltpu.SemaphoreType.DMA((5,)),
             pltpu.SemaphoreType.DMA((n_blocks,)),
         ],
         compiler_params=pltpu.CompilerParams(vmem_limit_bytes=58 << 20),

time: 120 us -> 122 us (1.017)
  Pallas kernels: 119 us -> 121 us
    pallas_call x1, Pallas kernels: 9.27 us -> 11.4 us  [late(): pl.pallas_call(functools.partial(late_kernel, n_grp, n_pts), out_shape=(j...]
where the time goes in v6:
time: 122 us
  Pallas kernels  121 us (99%)
    pallas_call x1, Pallas kernels, exchange(): pl.pallas_call(functools.partial(exchange_kernel, n_grp, n_pts), out_shap...  109 us
    pallas_call x1, Pallas kernels, late(): pl.pallas_call(functools.partial(late_kernel, n_grp, n_pts), out_shape=(j...  11.4 us

profile of v6, /device:TPU:1, one launch (start us, length us, event | category | flops | bytes accessed | tf_op | source)
XLA Modules:
  0.0 121.6 jit_solution(13746249550179118954)
XLA Ops:
  0.6 109.4 %exchange.1 = (bf16[16,1024,128]{2,1,0:T(8,128)(2,1)}, bf16[896,384]{1,0:T(8,128)(2,1)}, bf16[64,128,384]{2,1,0:T(8,128)(2,1)}, f32[64,128]{1,0:T(8,128)}) custom-call(s32[16,16]{1,0:T(8,128)} %counts.3, s32[3]{0:T(128)} %owner.3, s32[3,128]{1,0:T(4,128)} %slot_ref.3, bf16[1,1,16384,128]{3,2,1,0:T(8,128)(2,1)} %patches_ref.1), custom_call_target="tpu_custom_call" | custom-call | tf_op jit(solution)/shard_map/exchange/pallas_call | solution.py:482
  110.0 11.4 %late.1 = (bf16[1,1,8192,384]{3,2,1,0:T(8,128)(2,1)}, f32[64,128]{1,0:T(8,128)}) custom-call(s32[16,16]{1,0:T(8,128)} %counts.3, s32[3]{0:T(128)} %owner.3, s32[3,128]{1,0:T(4,128)} %slot_ref.3, bf16[16,1024,128]{2,1,0:T(8,128)(2,1)} %get-tuple-element.8.got_in, bf16[896,384]{1,0:T(8,128)(2,1)} %get-tuple-element.9.weights_ref, ...), custom_call_target="tpu_custom_call" | custom-call | tf_op jit(solution)/shard_map/late/pallas_call | solution.py:638
